TPU v7x, 256 devices: a whole 4x4x8 slice. The times are simulated.
256 devices in a mesh: win: 4 (over y_lo, core), tile: 64 (over x, y_hi, z).
Axes of the slice: x: 4, y: 4 (y_hi: 2, y_lo: 2; y = y_hi * 2 + y_lo), z: 8, core: 2. Of those that a mesh axis runs over, the one named last changes fastest.
Arguments:
- initial: float32 [4, 64, 36, 4096], P('win', 'tile'), may hold values from -6 to 6
- courant_x: bfloat16 [4, 64, 36, 4096], P('win', 'tile'), may hold values from 0.099609375 to 2.890625
- courant_y: bfloat16 [4, 64, 36, 4096], P('win', 'tile'), may hold values from 0.099609375 to 2.890625
- observed: float32 [4, 64, 64, 64], P('win', 'tile'), may hold values from -3 to 3
- precision_w: float32 [4, 64, 64, 64], P('win', 'tile'), may hold values from 0.2 to 2
- kernel: float32 [36], replicated, may hold values from 0.1 to 1
- profile: float32 [36], replicated, may hold values from 0.05 to 1
- emission: float32 [64, 64, 64], P('tile'), may hold values from -6 to 6
- edges: int32 [6, 64], replicated, may hold values from 0 to 63, as said below
Outputs:
- gradient: float32 [64, 64, 64], P('tile', 'win')
Inputs may be any that keep to these rules, and one draw needn't show every extreme that they name: edges[0, t] is (t - 1) or (t - 16) modulo 64, and edges[3, t] is (t - 2) or (t - 32) modulo 64; each of the four occurs for some tile; rows 1, 2, 4 and 5 hold 0 or 1, each value at some tile.
All inputs are finite; a program needn't handle non-finite values.
Results may differ from a plain program's by a relative error of at most 0.0003.
Values sent between devices are 32-bit elements; how exact they have to be, the bound alone decides.
A program may use at most 64 MiB of HBM per device.

v0:
```python
import jax
import jax.numpy as jnp
from jax import lax
from jax.sharding import PartitionSpec as P

STEPS = 2


def from_behind(block, axis, distance):
    devices = range(lax.axis_size(axis))
    route = [((i - distance) % len(devices), i) for i in devices]
    return lax.ppermute(block, axis, route)


def advect_along(tracer_field, rim_cells, courant, along):
    side_len = tracer_field.shape[along]
    extended = jnp.concatenate([rim_cells, tracer_field], along)
    edge_speed = lax.slice_in_dim(courant, side_len - 1, side_len, axis=along)
    inflow = jnp.zeros_like(tracer_field)
    outlet = jnp.zeros_like(edge_speed)
    for depth in range(1, 4):
        inflow = inflow + lax.slice_in_dim(
            extended, 3 - depth, 3 - depth + side_len, axis=along
        ) * jnp.clip(courant - (depth - 1), 0.0, 1.0)
        outlet = outlet + lax.slice_in_dim(
            tracer_field, side_len - depth, side_len - depth + 1, axis=along
        ) * jnp.clip(edge_speed - (depth - 1), 0.0, 1.0)
    outflow = jnp.concatenate([lax.slice_in_dim(inflow, 1, side_len, axis=along), outlet], along)
    return tracer_field - (outflow - inflow)


def advect_adjoint(sensitivity, courant, along):
    rim_shape = list(sensitivity.shape)
    rim_shape[along] = 3
    blank_field = jnp.zeros_like(sensitivity)
    blank_rim = jnp.zeros(tuple(rim_shape), jnp.float32)
    unused, pullback = jax.vjp(
        lambda tracer_field, rim_cells: advect_along(tracer_field, rim_cells, courant, along),
        blank_field,
        blank_rim,
    )
    return pullback(sensitivity)


def strips(tracer_field):
    side_len = tracer_field.shape[-1]
    east_strip = jnp.swapaxes(tracer_field[..., side_len - 3 :][..., ::-1], -1, -2)
    north_strip = tracer_field[..., side_len - 3 :, :][..., ::-1, :]
    return (east_strip, north_strip)


def add_strips(tracer_field_adjoint, east_bar, north_bar):
    side_len = tracer_field_adjoint.shape[-1]
    tracer_field_adjoint = tracer_field_adjoint.at[..., side_len - 3 :].add(
        jnp.swapaxes(east_bar, -1, -2)[..., ::-1]
    )
    return tracer_field_adjoint.at[..., side_len - 3 :, :].add(north_bar[..., ::-1, :])


def as_halo(panel, along):
    if along == 3:
        return jnp.swapaxes(panel[..., ::-1, :], -1, -2)
    return panel[..., ::-1, :]


def halo_back(rim_bar, along):
    if along == 3:
        return jnp.swapaxes(rim_bar, -1, -2)[..., ::-1, :]
    return rim_bar[..., ::-1, :]


def reverse_along(panel, flagged):
    return jnp.where(flagged, panel[..., ::-1], panel)


def own_entries(edges, position, base, tile_count, nearest):
    entries = lax.dynamic_slice_in_dim(edges, position, 1, 1)[:, 0]
    distant_indicator = entries[base] != (position - nearest) % tile_count
    return (distant_indicator, entries[base + 1], entries[base + 2])


def collect_receiver_index(tracer_field, local_details, shift_amounts, transfer_buffer):
    east_strip, north_strip = strips(tracer_field)
    stacked_panels = jnp.stack([east_strip, north_strip])
    received_neighbor = transfer_buffer(stacked_panels, shift_amounts[0])
    received_distant = transfer_buffer(stacked_panels, shift_amounts[1])
    distant_indicator, edge_code, flip_code = local_details
    arrived = jnp.where(distant_indicator, received_distant, received_neighbor)
    panel = jnp.where(edge_code == 0, arrived[0], arrived[1])
    return reverse_along(panel, flip_code == 1)


def backward_receiver_index(
    tracer_field_adjoint, panel_adjoint_value, local_details, shift_amounts, transfer_buffer
):
    distant_indicator, edge_code, flip_code = local_details
    returned = reverse_along(panel_adjoint_value, flip_code == 1)
    blank_panel = jnp.zeros_like(returned)
    stacked_panels = jnp.stack(
        [
            jnp.where(edge_code == 0, returned, blank_panel),
            jnp.where(edge_code == 0, blank_panel, returned),
        ]
    )
    empty_stacked_panels = jnp.zeros_like(stacked_panels)
    received_neighbor = transfer_buffer(
        jnp.where(distant_indicator, empty_stacked_panels, stacked_panels), -shift_amounts[0]
    )
    received_distant = transfer_buffer(
        jnp.where(distant_indicator, stacked_panels, empty_stacked_panels), -shift_amounts[1]
    )
    summed = received_neighbor + received_distant
    return add_strips(tracer_field_adjoint, summed[0], summed[1])


def body(initial, courant_x, courant_y, observed, precision_w, kernel, profile, emission, edges):
    side_len = observed.shape[-1]
    cube_shape = (initial.shape[0], initial.shape[2], side_len, side_len)
    tracer = initial[:, 0].reshape(cube_shape)
    speed_x = courant_x[:, 0].astype(jnp.float32).reshape(cube_shape)
    speed_y = courant_y[:, 0].astype(jnp.float32).reshape(cube_shape)
    source_rate = profile[None, :, None, None] * emission[0][None, None]
    tile_count = lax.axis_size("tile")
    position = lax.axis_index("tile")
    offsets_x = (1, tile_count // 4)
    offsets_y = (2, tile_count // 2)
    own_x = own_entries(edges, position, 0, tile_count, 1)
    own_y = own_entries(edges, position, 3, tile_count, 2)

    def carry_x(payload, offset):
        return from_behind(payload, "tile", offset)

    def carry_y(payload, offset):
        return from_behind(payload, "tile", offset)

    def return_x(payload, offset):
        return from_behind(payload, "tile", offset)

    def return_y(payload, offset):
        return from_behind(payload, "tile", offset)

    for step_index in range(STEPS):
        tracer = advect_along(
            tracer,
            as_halo(collect_receiver_index(tracer, own_x, offsets_x, carry_x), 3),
            speed_x,
            3,
        )
        tracer = advect_along(
            tracer,
            as_halo(collect_receiver_index(tracer, own_y, offsets_y, carry_y), 2),
            speed_y,
            2,
        )
        tracer = tracer + source_rate
    weight_sum = jnp.sum(kernel)
    column = jnp.sum(kernel[None, :, None, None] * tracer, axis=1) / weight_sum
    misfit = column - observed[:, 0]
    adjoint = (precision_w[:, 0] * misfit)[:, None] * (kernel[None, :, None, None] / weight_sum)
    gradient = jnp.zeros(emission.shape[1:], jnp.float32)
    for step_index in range(STEPS):
        gradient = gradient + jnp.sum(profile[None, :, None, None] * adjoint, axis=(0, 1))
        if step_index + 1 < STEPS:
            adjoint, rim_bar = advect_adjoint(adjoint, speed_y, 2)
            adjoint = backward_receiver_index(
                adjoint, halo_back(rim_bar, 2), own_y, offsets_y, return_y
            )
            adjoint, rim_bar = advect_adjoint(adjoint, speed_x, 3)
            adjoint = backward_receiver_index(
                adjoint, halo_back(rim_bar, 3), own_x, offsets_x, return_x
            )
    summed_all = lax.psum(gradient, "win")
    row_count = gradient.shape[0] // lax.axis_size("win")
    share_rows = lax.dynamic_slice_in_dim(
        summed_all, lax.axis_index("win") * row_count, row_count, 0
    )
    return share_rows[None]


def solution(mesh):
    placed = (
        P("win", "tile", None, None),
        P("win", "tile", None, None),
        P("win", "tile", None, None),
        P("win", "tile", None, None),
        P("win", "tile", None, None),
        P(),
        P(),
        P("tile", None, None),
        P(),
    )
    return jax.shard_map(
        body, mesh=mesh, in_specs=placed, out_specs=P("tile", "win", None), check_vma=False
    )
```

profile of v0, /device:TPU:1, one launch (start us, length us, event | category | flops | bytes accessed | tf_op | source)
XLA Modules:
  0.0 279.1 jit_solution(16219852052872074876)
XLA Ops:
  0.0 2.5 reduce.9
  7.3 2.1 collective-permute-start
  9.4 2.1 collective-permute-start.1
  17.1 2.3 copy.185
  19.4 2.4 collective-permute-done.1
  21.8 2.4 copy.186
  27.5 3.3 %rev.75 = f32[1,36,3,64]{2,1,3,0:T(8,128)} reverse(f32[1,36,3,64]{2,1,3,0:T(8,128)} %reverse_select_fusion.1), dimensions={2} | reverse | bytes 55296 | tf_op jit(solution)/shard_map/rev | solution.py:62
  30.8 5.5 %fusion.53 = (f32[1,36,64,64]{3,1,2,0:T(8,128)S(1)}, f32[1,36,64,64]{3,1,2,0:T(8,128)}) fusion(f32[1,36,64,64]{3,2,0,1:T(8,128)} %reshape.545, f32[1,36,64,64]{3,1,2,0:T(8,128)S(1)} %copy.200, f32[1,36,64,3]{3,1,2,0:T(8,128)} %bitcast.80), kind=kLoop, calls=%fused_computation.160 | loop fusion | flops 1916928 | bytes 2386944 | tf_op jit(solution)/shard_map/convert_element_type | solution.py:120
  41.1 2.8 %fusion.24 = f32[1,36,64,1]{3,1,2,0:T(8,128)S(1)} fusion(f32[1,36,64,1]{3,1,2,0:T(8,128)} %copy.199, f32[1,36,64,64]{3,1,2,0:T(8,128)S(1)} %copy.200, f32[1,36,64,64]{3,1,2,0:T(8,128)S(1)} %get-tuple-element.82), kind=kLoop, calls=%fused_computation.53 | loop fusion | flops 18432 | bytes 55296 | tf_op jit(solution)/shard_map/add | solution.py:25
  56.8 7.5 %collective-permute-done.3 = f32[2,1,36,3,64]{4,2,3,1,0:T(8,128)S(1)} collective-permute-done((f32[2,1,36,3,64]{4,2,3,1,0:T(8,128)S(1)}, f32[2,1,36,3,64]{4,2,3,1,0:T(8,128)S(1)}, u32[]{:S(2)}, u32[]{:S(2)}) %collective-permute-start.3) | collective-permute-done | bytes 55328 | tf_op jit(solution)/shard_map/ppermute | solution.py:12
  64.4 2.2 fusion.52
  72.3 3.8 %fusion.17 = f32[1,36,64,1]{3,1,2,0:T(8,128)} fusion(f32[1,36,64,1]{3,1,2,0:T(8,128)} %copy.199, f32[1,36,64,64]{3,1,2,0:T(8,128)S(1)} %multiply_add_fusion.1, f32[1,36,64,64]{3,1,2,0:T(8,128)S(1)} %get-tuple-element.82), kind=kLoop, calls=%fused_computation.38 | loop fusion | flops 18432 | bytes 55296 | tf_op jit(solution)/shard_map/add | solution.py:25
  77.2 2.4 copy.208
  79.5 2.2 collective-permute-done.5
  81.8 2.4 copy.209
  87.5 3.3 %rev.83 = f32[1,36,3,64]{2,1,3,0:T(8,128)} reverse(f32[1,36,3,64]{2,1,3,0:T(8,128)} %reverse_select_fusion), dimensions={2} | reverse | bytes 55296 | tf_op jit(solution)/shard_map/rev | solution.py:62
  90.8 4.4 %fusion.20 = f32[1,36,64,64]{3,1,2,0:T(8,128)S(1)} fusion(f32[1,36,64,64]{3,1,2,0:T(8,128)S(1)} %multiply_add_fusion.1, f32[1,36,64,3]{3,1,2,0:T(8,128)} %bitcast.79, f32[1,36,64,64]{3,2,0,1:T(8,128)} %reshape.545), kind=kLoop, calls=%fused_computation.44 | loop fusion | flops 1916928 | bytes 1797120 | tf_op jit(solution)/shard_map/add | solution.py:22
  101.6 4.2 %collective-permute-done.6 = f32[2,1,36,3,64]{4,2,3,1,0:T(8,128)S(1)} collective-permute-done((f32[2,1,36,3,64]{4,2,3,1,0:T(8,128)S(1)}, f32[2,1,36,3,64]{4,2,3,1,0:T(8,128)S(1)}, u32[]{:S(2)}, u32[]{:S(2)}) %collective-permute-start.6) | collective-permute-done | bytes 55328 | tf_op jit(solution)/shard_map/ppermute | solution.py:12
  105.8 5.5 %collective-permute-done.7 = f32[2,1,36,3,64]{4,2,3,1,0:T(8,128)S(1)} collective-permute-done((f32[2,1,36,3,64]{4,2,3,1,0:T(8,128)S(1)}, f32[2,1,36,3,64]{4,2,3,1,0:T(8,128)S(1)}, u32[]{:S(2)}, u32[]{:S(2)}) %collective-permute-start.7) | collective-permute-done | bytes 55328 | tf_op jit(solution)/shard_map/ppermute | solution.py:12
  111.5 3.3 %fusion.5 = (f32[1,36,64,64]{3,1,2,0:T(8,128)S(1)}, f32[1,36,64,64]{3,1,2,0:T(8,128)}) fusion(f32[1,36,64,64]{3,1,2,0:T(8,128)S(1)} %copy-done.5, f32[1,36,3,64]{3,1,2,0:T(8,128)S(1)} %rev.87, f32[1,36,64,64]{3,2,0,1:T(8,128)} %reshape.546), kind=kLoop, calls=%fused_computation.20 | loop fusion | flops 1916928 | bytes 2386944 | tf_op jit(solution)/shard_map/add | solution.py:22
  121.6 2.9 %copy.219 = f32[1,36,64,64]{2,1,3,0:T(8,128)} copy(f32[1,36,64,64]{3,1,2,0:T(8,128)} %get-tuple-element.79) | data formatting | bytes 1179648 | tf_op jit(solution)/shard_map/jit(clip)/min | solution.py:24
  126.1 3.6 %fusion.51 = (f32[1,36,64,64]{2,1,3,0:T(8,128)}, f32[1,36,64,64]{2,1,3,0:T(8,128)}) fusion(f32[1,36,64,64]{2,1,3,0:T(8,128)} %copy.219, f32[1,36,63,64]{2,1,3,0:T(8,128)} %copy.271, f32[36]{0:T(128)S(1)} %broadcast_divide_fusion, f32[64,64]{0,1:T(8,128)S(1)} %copy.212), kind=kLoop, calls=%fused_computation.158 | loop fusion | flops 442368 | bytes 2366608 | tf_op jit(solution)/shard_map/transpose(jvp())/mul | solution.py:22
  129.7 2.9 %copy.217 = f32[1,36,64,64]{3,1,2,0:T(8,128)} copy(f32[1,36,64,64]{2,1,3,0:T(8,128)} %get-tuple-element.56) | data formatting | bytes 1179648 | tf_op jit(solution)/shard_map/transpose(jvp())/add_any | solution.py:28
  132.6 2.2 fusion.39
  136.6 2.1 pad_add_fusion.6
  140.2 2.6 rev.88
  142.8 2.6 rev.89
  145.4 2.9 %copy.250 = f32[1,36,64,64]{3,1,2,0:T(8,128)} copy(f32[1,36,64,64]{2,1,3,0:T(8,128)} %split.34) | data formatting | bytes 1179648
  149.8 2.7 pad_maximum_fusion
  152.5 2.5 copy.228
  157.0 2.6 copy.225
  167.1 17.9 %scatter-add.14 = f32[1,36,64,64]{3,1,2,0:T(8,128)S(1)} dynamic-update-slice(f32[1,36,64,64]{3,1,2,0:T(8,128)S(1)} %add_add_fusion, f32[1,36,64,3]{3,1,2,0:T(8,128)} %copy.231, s32[]{:T(128)} %constant.141.clone.1, s32[]{:T(128)} %constant.141.clone.1, s32[]{:T(128)} %constant.141.clone.1, s32[]{:T(128)} %constant.153.clone.1) | dynamic-update-slice | bytes 55300 | tf_op jit(solution)/shard_map/scatter-add | solution.py:54
  187.8 4.1 %fusion.40 = (f32[1,36,64,1]{3,1,2,0:T(8,128)}, f32[1,36,64,1]{3,1,2,0:T(8,128)}, f32[1,36,64,1]{3,1,2,0:T(8,128)}) fusion(f32[1,36,64,64]{3,1,2,0:T(8,128)S(1)} %get-tuple-element.82, f32[1,36,64,64]{3,1,2,0:T(8,128)} %neg.17), kind=kLoop, calls=%fused_computation.103 | loop fusion | flops 11520 | bytes 46080 | tf_op jit(solution)/shard_map/transpose(jvp())/mul | solution.py:25
  195.3 2.6 rev.92
  198.0 2.6 rev.93
  206.6 2.7 fusion
  209.2 2.5 copy.238
  211.8 3.6 %collective-permute-start.10 = (f32[2,1,36,3,64]{4,0,3,2,1:T(2,128)S(1)}, f32[2,1,36,3,64]{4,0,3,2,1:T(2,128)S(1)}, u32[]{:S(2)}, u32[]{:S(2)}) collective-permute-start(f32[2,1,36,3,64]{4,0,3,2,1:T(2,128)S(1)} %copy.238), channel_id=1, source_target_pairs={{1,0},{2,1},{3,2},{4,3},{5,4},{6,5},{7,6},{8,7},{9,8},{10,9},{11,1... | collective-permute-start | bytes 165896 | tf_op jit(solution)/shard_map/ppermute | solution.py:12
  215.3 2.6 copy.239
  222.3 2.3 copy.240
  224.6 2.4 copy.241
  227.0 2.8 %add.201 = f32[2,1,36,3,64]{3,2,4,1,0:T(8,128)S(1)} add(f32[2,1,36,3,64]{3,2,4,1,0:T(8,128)} %copy.240, f32[2,1,36,3,64]{3,2,4,1,0:T(8,128)} %copy.241) | non-fusion elementwise | flops 13824 | bytes 165888 | tf_op jit(solution)/shard_map/add | solution.py:112
  231.0 3.3 %rev.94 = f32[1,36,64,3]{3,1,2,0:T(8,128)} reverse(f32[1,36,64,3]{3,1,2,0:T(8,128)} %get-tuple-element.61), dimensions={3} | reverse | bytes 55296 | tf_op jit(solution)/shard_map/rev | solution.py:55
  234.3 2.9 %add.202 = f32[1,36,64,3]{3,1,2,0:T(8,128)} add(f32[1,36,64,3]{3,1,2,0:T(8,128)} %copy.252, f32[1,36,64,3]{3,1,2,0:T(8,128)} %rev.94) | non-fusion elementwise | flops 6912 | bytes 82944 | tf_op jit(solution)/shard_map/add | solution.py:54
  239.0 2.6 rev.95
  241.6 2.8 %slice_add_fusion = f32[1,36,3,64]{2,1,3,0:T(8,128)} fusion(f32[1,36,3,64]{2,1,3,0:T(8,128)} %rev.95, f32[1,36,64,64]{2,1,3,0:T(8,128)S(1)} %constant_dynamic-update-slice_fusion), kind=kLoop, calls=%fused_computation.32 | loop fusion | flops 6912 | bytes 82944 | tf_op jit(solution)/shard_map/add | solution.py:57
  244.4 18.0 %scatter-add.19 = f32[1,36,64,64]{2,1,3,0:T(8,128)S(1)} dynamic-update-slice(f32[1,36,64,64]{2,1,3,0:T(8,128)S(1)} %constant_dynamic-update-slice_fusion, f32[1,36,3,64]{2,1,3,0:T(8,128)} %slice_add_fusion, s32[]{:T(128)} %constant.141.clone.1, s32[]{:T(128)} %constant.141.clone.1, s32[]{:T(128)} %constant.153.clone.1, s32[]{:T(128)} %constant.141.clone.1) | dynamic-update-slice | bytes 55300 | tf_op jit(solution)/shard_map/scatter-add | solution.py:57
  263.0 15.2 %psum.7 = f32[64,64]{0,1:T(8,128)S(1)} all-reduce(f32[64,64]{0,1:T(8,128)S(1)} %add.204), channel_id=1, replica_groups=mesh['win'=4,'tile'=64] {'win'}, use_global_device_ids=true, to_apply=%region_4.5 | all-reduce | flops 4096 | bytes 32768 | tf_op jit(solution)/shard_map/psum | solution.py:172
  (182 shorter events, 87.2 us)
Async XLA Ops:
  0.0 11.6 %copy-start = (s32[6,64]{1,0:T(8,128)S(1)}, s32[6,64]{1,0:T(8,128)}, u32[]{:S(2)}) copy-start(s32[6,64]{1,0:T(8,128)} %param.25) | copy-start | bytes 4612
  3.0 9.3 %copy-start.6 = (f32[1,36,64,64]{3,2,0,1:T(8,128)}, f32[1,36,64,64]{3,2,0,1:T(8,128)S(1)}, u32[]{:S(2)}) copy-start(f32[1,36,64,64]{3,2,0,1:T(8,128)S(1)} %reshape_squeeze.3) | copy-start | bytes 1769476
  7.3 5.7 %copy-start.22 = (bf16[1,1,36,4096]{3,2,1,0:T(8,128)(2,1)S(1)}, bf16[1,1,36,4096]{3,2,1,0:T(8,128)(2,1)}, u32[]{:S(2)}) copy-start(bf16[1,1,36,4096]{3,2,1,0:T(8,128)(2,1)} %param.18) | copy-start | bytes 884740
  7.3 9.8 %collective-permute-start = (f32[2,1,36,3,64]{4,0,3,2,1:T(2,128)S(1)}, f32[2,1,36,3,64]{4,0,3,2,1:T(2,128)S(1)}, u32[]{:S(2)}, u32[]{:S(2)}) collective-permute-start(f32[2,1,36,3,64]{4,0,3,2,1:T(2,128)S(1)} %pad_maximum_fusion.9), channel_id=1, source_target_pairs={{48,0},{49,1},{50,2},{51,3},{52,4},{53,5},{54,6},{55,7},{56,8},{57... | collective-permute-start | bytes 165896 | tf_op jit(solution)/shard_map/ppermute | solution.py:12
  9.4 12.4 %collective-permute-start.1 = (f32[2,1,36,3,64]{4,0,3,2,1:T(2,128)S(1)}, f32[2,1,36,3,64]{4,0,3,2,1:T(2,128)S(1)}, u32[]{:S(2)}, u32[]{:S(2)}) collective-permute-start(f32[2,1,36,3,64]{4,0,3,2,1:T(2,128)S(1)} %pad_maximum_fusion.9), channel_id=1, source_target_pairs={{63,0},{0,1},{1,2},{2,3},{3,4},{4,5},{5,6},{6,7},{7,8},{8,9},{9,10... | collective-permute-start | bytes 165896 | tf_op jit(solution)/shard_map/ppermute | solution.py:12
  13.0 3.5 %copy-start.28 = (f32[36]{0:T(128)S(1)}, f32[36]{0:T(128)}, u32[]{:S(2)}) copy-start(f32[36]{0:T(128)} %param.22) | copy-start | bytes 436
  41.1 2.8 %copy-start.11 = (f32[1,36,64,64]{3,1,2,0:T(8,128)S(1)}, f32[1,36,64,64]{3,1,2,0:T(8,128)}, u32[]{:S(2)}) copy-start(f32[1,36,64,64]{3,1,2,0:T(8,128)} %get-tuple-element.83) | copy-start | bytes 1769476
  44.0 1.3 copy-start.7
  46.1 20.6 %copy-start.2 = (f32[1,36,64,64]{3,1,2,0:T(8,128)}, f32[1,36,64,64]{3,1,2,0:T(8,128)S(1)}, u32[]{:S(2)}) copy-start(f32[1,36,64,64]{3,1,2,0:T(8,128)S(1)} %fusion.30) | copy-start | bytes 1769476
  47.6 5.8 %copy-start.23 = (bf16[1,1,36,4096]{3,2,1,0:T(8,128)(2,1)S(1)}, bf16[1,1,36,4096]{3,2,1,0:T(8,128)(2,1)}, u32[]{:S(2)}) copy-start(bf16[1,1,36,4096]{3,2,1,0:T(8,128)(2,1)} %param.19) | copy-start | bytes 884740
  49.5 7.3 %collective-permute-start.2 = (f32[2,1,36,3,64]{4,2,3,1,0:T(8,128)S(1)}, f32[2,1,36,3,64]{4,2,3,1,0:T(8,128)S(1)}, u32[]{:S(2)}, u32[]{:S(2)}) collective-permute-start(f32[2,1,36,3,64]{4,2,3,1,0:T(8,128)S(1)} %pad_maximum_fusion.6), channel_id=1, source_target_pairs={{32,0},{33,1},{34,2},{35,3},{36,4},{37,5},{38,6},{39,7},{40,8},{41... | collective-permute-start | bytes 165896 | tf_op jit(solution)/shard_map/ppermute | solution.py:12
  51.1 13.2 %collective-permute-start.3 = (f32[2,1,36,3,64]{4,2,3,1,0:T(8,128)S(1)}, f32[2,1,36,3,64]{4,2,3,1,0:T(8,128)S(1)}, u32[]{:S(2)}, u32[]{:S(2)}) collective-permute-start(f32[2,1,36,3,64]{4,2,3,1,0:T(8,128)S(1)} %pad_maximum_fusion.6), channel_id=1, source_target_pairs={{62,0},{63,1},{0,2},{1,3},{2,4},{3,5},{4,6},{5,7},{6,8},{7,9},{8,1... | collective-permute-start | bytes 165896 | tf_op jit(solution)/shard_map/ppermute | solution.py:12
  66.7 1.1 copy-start.21
  66.7 1.8 copy-start.3
  66.7 1.8 copy-start.24
  66.7 1.8 copy-start.27
  72.2 5.0 %collective-permute-start.4 = (f32[2,1,36,3,64]{4,2,3,1,0:T(8,128)S(1)}, f32[2,1,36,3,64]{4,2,3,1,0:T(8,128)S(1)}, u32[]{:S(2)}, u32[]{:S(2)}) collective-permute-start(f32[2,1,36,3,64]{4,2,3,1,0:T(8,128)S(1)} %pad_maximum_fusion.7), channel_id=1, source_target_pairs={{48,0},{49,1},{50,2},{51,3},{52,4},{53,5},{54,6},{55,7},{56,8},{57... | collective-permute-start | bytes 165896 | tf_op jit(solution)/shard_map/ppermute | solution.py:12
  72.2 9.5 %collective-permute-start.5 = (f32[2,1,36,3,64]{4,2,3,1,0:T(8,128)S(1)}, f32[2,1,36,3,64]{4,2,3,1,0:T(8,128)S(1)}, u32[]{:S(2)}, u32[]{:S(2)}) collective-permute-start(f32[2,1,36,3,64]{4,2,3,1,0:T(8,128)S(1)} %pad_maximum_fusion.7), channel_id=1, source_target_pairs={{63,0},{0,1},{1,2},{2,3},{3,4},{4,5},{5,6},{6,7},{7,8},{8,9},{9,10... | collective-permute-start | bytes 165896 | tf_op jit(solution)/shard_map/ppermute | solution.py:12
  95.3 1.3 copy-start.20
  97.1 1.5 copy-start.4
  98.6 2.3 copy-start.5
  100.5 5.3 %collective-permute-start.6 = (f32[2,1,36,3,64]{4,2,3,1,0:T(8,128)S(1)}, f32[2,1,36,3,64]{4,2,3,1,0:T(8,128)S(1)}, u32[]{:S(2)}, u32[]{:S(2)}) collective-permute-start(f32[2,1,36,3,64]{4,2,3,1,0:T(8,128)S(1)} %pad_maximum_fusion.8), channel_id=1, source_target_pairs={{32,0},{33,1},{34,2},{35,3},{36,4},{37,5},{38,6},{39,7},{40,8},{41... | collective-permute-start | bytes 165896 | tf_op jit(solution)/shard_map/ppermute | solution.py:12
  100.6 10.7 %collective-permute-start.7 = (f32[2,1,36,3,64]{4,2,3,1,0:T(8,128)S(1)}, f32[2,1,36,3,64]{4,2,3,1,0:T(8,128)S(1)}, u32[]{:S(2)}, u32[]{:S(2)}) collective-permute-start(f32[2,1,36,3,64]{4,2,3,1,0:T(8,128)S(1)} %pad_maximum_fusion.8), channel_id=1, source_target_pairs={{62,0},{63,1},{0,2},{1,3},{2,4},{3,5},{4,6},{5,7},{6,8},{7,9},{8,1... | collective-permute-start | bytes 165896 | tf_op jit(solution)/shard_map/ppermute | solution.py:12
  114.9 0.8 copy-start.25
  114.9 0.8 copy-start.26
  119.4 1.1 copy-start.10
  120.5 1.1 copy-start.14
  121.6 2.9 %slice-start = ((f32[1,36,64,64]{3,1,2,0:T(8,128)}), f32[1,36,63,64]{3,1,2,0:T(8,128)S(1)}, s32[]{:S(2)}) async-start(f32[1,36,64,64]{3,1,2,0:T(8,128)} %copy-done.14), calls=%async_computation | async-start | bytes 2580480 | tf_op jit(solution)/shard_map/transpose(jvp())/split | solution.py:28
  129.7 2.9 %copy-start.8 = (f32[1,36,64,64]{3,2,0,1:T(8,128)S(1)}, f32[1,36,64,64]{3,2,0,1:T(8,128)}, u32[]{:S(2)}) copy-start(f32[1,36,64,64]{3,2,0,1:T(8,128)} %reshape.546) | copy-start | bytes 1769476
  145.4 3.0 %copy-start.18 = (f32[1,36,3,64]{2,1,3,0:T(8,128)S(1)}, f32[1,36,3,64]{2,1,3,0:T(8,128)}, u32[]{:S(2)}) copy-start(f32[1,36,3,64]{2,1,3,0:T(8,128)} %rev.88) | copy-start | bytes 82948
  155.0 10.4 %collective-permute-start.9 = (f32[2,1,36,3,64]{4,0,3,2,1:T(2,128)S(1)}, f32[2,1,36,3,64]{4,0,3,2,1:T(2,128)S(1)}, u32[]{:S(2)}, u32[]{:S(2)}) collective-permute-start(f32[2,1,36,3,64]{4,0,3,2,1:T(2,128)S(1)} %copy.228), channel_id=1, source_target_pairs={{32,0},{33,1},{34,2},{35,3},{36,4},{37,5},{38,6},{39,7},{40,8},{41... | collective-permute-start | bytes 165896 | tf_op jit(solution)/shard_map/ppermute | solution.py:12
  159.7 5.8 %collective-permute-start.8 = (f32[2,1,36,3,64]{4,0,3,2,1:T(2,128)S(1)}, f32[2,1,36,3,64]{4,0,3,2,1:T(2,128)S(1)}, u32[]{:S(2)}, u32[]{:S(2)}) collective-permute-start(f32[2,1,36,3,64]{4,0,3,2,1:T(2,128)S(1)} %copy.226), channel_id=1, source_target_pairs={{2,0},{3,1},{4,2},{5,3},{6,4},{7,5},{8,6},{9,7},{10,8},{11,9},{12,... | collective-permute-start | bytes 165896 | tf_op jit(solution)/shard_map/ppermute | solution.py:12
  187.8 4.1 %copy-start.9 = (f32[1,36,64,64]{3,2,0,1:T(8,128)S(1)}, f32[1,36,64,64]{3,2,0,1:T(8,128)}, u32[]{:S(2)}) copy-start(f32[1,36,64,64]{3,2,0,1:T(8,128)} %reshape.545) | copy-start | bytes 1769476
  187.8 4.1 %copy-start.12 = (f32[1,36,64,64]{3,1,2,0:T(8,128)S(1)}, f32[1,36,64,64]{3,1,2,0:T(8,128)}, u32[]{:S(2)}) copy-start(f32[1,36,64,64]{3,1,2,0:T(8,128)} %neg.17) | copy-start | bytes 1769476
  198.0 2.6 copy-start.15
  200.6 1.6 copy-start.19
  202.7 3.7 %copy-start.16 = (f32[1,36,3,64]{2,1,3,0:T(8,128)S(1)}, f32[1,36,3,64]{2,1,3,0:T(8,128)}, u32[]{:S(2)}) copy-start(f32[1,36,3,64]{2,1,3,0:T(8,128)} %rev.92) | copy-start | bytes 82948
  202.7 3.7 %copy-start.17 = (f32[1,36,3,64]{2,1,3,0:T(8,128)S(1)}, f32[1,36,3,64]{2,1,3,0:T(8,128)}, u32[]{:S(2)}) copy-start(f32[1,36,3,64]{2,1,3,0:T(8,128)} %rev.93) | copy-start | bytes 82948
  211.8 10.5 %collective-permute-start.10 = (f32[2,1,36,3,64]{4,0,3,2,1:T(2,128)S(1)}, f32[2,1,36,3,64]{4,0,3,2,1:T(2,128)S(1)}, u32[]{:S(2)}, u32[]{:S(2)}) collective-permute-start(f32[2,1,36,3,64]{4,0,3,2,1:T(2,128)S(1)} %copy.238), channel_id=1, source_target_pairs={{1,0},{2,1},{3,2},{4,3},{5,4},{6,5},{7,6},{8,7},{9,8},{10,9},{11,1... | collective-permute-start | bytes 165896 | tf_op jit(solution)/shard_map/ppermute | solution.py:12
  215.3 3.9 %copy-start.13 = (f32[1,36,64,64]{2,1,3,0:T(8,128)S(1)}, f32[1,36,64,64]{2,1,3,0:T(8,128)}, u32[]{:S(2)}) copy-start(f32[1,36,64,64]{2,1,3,0:T(8,128)} %copy.233) | copy-start | bytes 1769476
  218.0 6.6 %collective-permute-start.11 = (f32[2,1,36,3,64]{4,0,3,2,1:T(2,128)S(1)}, f32[2,1,36,3,64]{4,0,3,2,1:T(2,128)S(1)}, u32[]{:S(2)}, u32[]{:S(2)}) collective-permute-start(f32[2,1,36,3,64]{4,0,3,2,1:T(2,128)S(1)} %copy.239), channel_id=1, source_target_pairs={{16,0},{17,1},{18,2},{19,3},{20,4},{21,5},{22,6},{23,7},{24,8},{25... | collective-permute-start | bytes 165896 | tf_op jit(solution)/shard_map/ppermute | solution.py:12
  244.4 34.5 %copy-start.1 = (s32[6,64]{1,0:T(8,128)S(1)}, s32[6,64]{1,0:T(8,128)}, u32[]{:S(2)}) copy-start(s32[6,64]{1,0:T(8,128)} %param.25) | copy-start | bytes 4612
where the time goes:
time: 284 us; the launch traced here: 279 us
  local copies, waits for them, and re-layouts  146 us (51%)
  other arithmetic  74.5 us (26%)
  waiting for transfers between devices  22.9 us (8%)
  starting transfers between devices  15.6 us (5%)
  blocking collectives  15.2 us (5%)
  between operations  4.62 us (2%)
    ppermute x12, waiting for transfers between devices, from_behind(): return lax.ppermute(block, axis, route)  22.9 us
    unnamed x67, local copies, waits for them, and re-layouts  20.8 us
    scatter-add x2, local copies, waits for them, and re-layouts, add_strips(): tracer_field_adjoint.at[..., side_len - 3:, :].add(north_bar[..., ::-1, :])  19.5 us
    scatter-add x2, local copies, waits for them, and re-layouts, add_strips(): tracer_field_adjoint.at[..., side_len - 3:]  17.9 us
    ppermute x12, starting transfers between devices, from_behind(): return lax.ppermute(block, axis, route)  15.6 us
    psum x1, blocking collectives, body(): summed_all = lax.psum(gradient, 'win')  15.2 us
    ppermute x6, local copies, waits for them, and re-layouts, from_behind(): return lax.ppermute(block, axis, route)  14.1 us
    add x2, other arithmetic, advect_along(): inflow + lax.slice_in_dim(extended, 3 - depth, 3 - depth + side_len, axis...  7.73 us
  transfers between devices with their start and end apart: 12, of which 6 were waited for; matrix products, arithmetic and copies ran while one was open for 11% of the time, Pallas kernels for 0%

commit v1 on v0

v1 whole, which is shorter than its diff:
```python
import jax
import jax.numpy as jnp
from jax import lax
from jax.experimental import pallas as pl
from jax.experimental.pallas import tpu as pltpu
from jax.sharding import PartitionSpec as P

F32 = jnp.float32
BF16 = jnp.bfloat16
I32 = jnp.int32
SIDE = 64
LANES = 128
CELLS = SIDE * SIDE
NV = CELLS // LANES
MESH = pl.DeviceIdType.MESH


def roll(x, shift):
    return pltpu.roll(x, shift % LANES, 1)


def lanes_of(shape):
    return lax.broadcasted_iota(I32, shape, 1)


def coefs(c):
    return jnp.clip(c, 0.0, 1.0), jnp.clip(c - 1.0, 0.0, 1.0), jnp.clip(c - 2.0, 0.0, 1.0)


def chunk(v):
    if isinstance(v, int):
        return pl.ds(v * LANES, LANES)
    return pl.ds(pl.multiple_of(v * LANES, LANES), LANES)


def slot_key(index):
    part = index & 3
    cell = 32 * (index >> 7) + 2 * ((index >> 2) & 15) + ((index >> 6) & 1)
    return part * SIDE + cell, part < 3


def north_key(index):
    return index - SIDE, index >= SIDE


def make_kernel(levels, windows):
    rows = (levels + 7) // 8 * 8
    per = NV // windows

    def kernel(
        init_h, cx_h, cy_h, obs_h, pre_h, ker_h, pro_h, emi_h, edges,
        out,
        qi, q, bx, mu, cx, cy, cxb, cyb, sq, sq2, flat, kp, kcol, pcol, gf,
        wx, wxt, wy, wyt, epack, cpack, dbuf,
        sbuf, rbuf, sset, rset, scol, rcol, spb, rpb, gint, rg, fin,
        in_sem, s_sem, r_sem, sset_sem, rset_sem, scol_sem, rcol_sem, spb_sem, rpb_sem, sg_sem, rg_sem,
    ):
        w = lax.axis_index("win")
        t = lax.axis_index("tile")
        tiles = lax.axis_size("tile")
        off_x = (1, tiles // 4)
        off_y = (2, tiles // 2)

        def fwd(off):
            return lax.rem(t + off, tiles)

        def bwd(off):
            return lax.rem(t + tiles - off, tiles)

        def win_of(r):
            return lax.rem(w + r, windows)

        loads = [
            pltpu.make_async_copy(init_h, qi, in_sem.at[0]),
            pltpu.make_async_copy(cx_h.at[0, 0], cxb, in_sem.at[1]),
            pltpu.make_async_copy(cy_h.at[0, 0], cyb, in_sem.at[2]),
            pltpu.make_async_copy(ker_h, kp.at[0], in_sem.at[3]),
            pltpu.make_async_copy(pro_h, kp.at[1], in_sem.at[4]),
            pltpu.make_async_copy(emi_h.at[0], sq.at[0], in_sem.at[5]),
            pltpu.make_async_copy(obs_h.at[0, 0], sq.at[1], in_sem.at[6]),
            pltpu.make_async_copy(pre_h.at[0, 0], sq.at[2], in_sem.at[7]),
        ]
        for load in loads:
            load.start()

        barrier = pltpu.get_barrier_semaphore()
        partners = []
        near = {1, tiles // 4, tiles - 1, tiles - tiles // 4}
        far = near | {2, tiles - 2, tiles // 2}
        for off in sorted(far):
            partners.append((w, fwd(off)))
        for r in range(1, windows):
            for off in sorted(near | {0}):
                partners.append((win_of(r), fwd(off)))
        for who in partners:
            pl.semaphore_signal(barrier, inc=1, device_id=who, device_id_type=MESH)

        lane = lanes_of((rows, LANES))
        l64 = lane & (SIDE - 1)
        low = lane < SIDE
        lane8 = lanes_of((8, LANES))
        l64_8 = lane8 & (SIDE - 1)
        low8 = lane8 < SIDE
        lane1 = lanes_of((1, LANES))
        low1 = lane1 < SIDE

        row_index = lax.broadcasted_iota(I32, (256, LANES), 0)

        def rows_key(kind):
            key, valid = (slot_key if kind == 0 else north_key)(row_index)
            return jnp.where(valid, key, -1000)

        def cols_key(kind, half):
            key, valid = (slot_key if kind == 0 else north_key)(lane1 + half * LANES)
            return jnp.where(valid, key, -2000)

        def choices(base, offs):
            out_ = []
            for off in offs:
                to = fwd(off)
                mine = (edges[base, to] == t).astype(I32)
                code = edges[base + 1, to]
                flip = edges[base + 2, to]
                out_.append((63 * flip, 4096 * (1 - mine * (1 - code)), 4096 * (1 - mine * code)))
            return out_

        row_keys = (rows_key(0), rows_key(1))

        def hot(mask):
            return jnp.where(mask, 1.0, 0.0).astype(BF16)

        def build(mat, base, offs, kind, transposed):
            for d, (flip, not_east, not_north) in enumerate(choices(base, offs)):
                for src in range(2):
                    away = not_east if src == 0 else not_north
                    for half in range(2):
                        if transposed:
                            cols = (cols_key(src, half) ^ flip) + away
                            mat[pl.ds(d * 256, 256), pl.ds(src * 256 + half * LANES, LANES)] = hot(row_keys[kind] == cols)
                        else:
                            cols = (cols_key(kind, half) ^ flip) + away
                            mat[pl.ds(src * 256, 256), pl.ds(d * 256 + half * LANES, LANES)] = hot(row_keys[src] == cols)

        def permute(x, mat):
            top = x.astype(BF16).astype(F32)
            both = jnp.concatenate([top, x - top], axis=0).astype(BF16)
            res = jnp.dot(both, mat[...], preferred_element_type=F32)
            n = x.shape[0]
            return res[:n] + res[n:]

        def send(stage, d, to):
            copy = pltpu.make_async_remote_copy(
                src_ref=sbuf.at[stage, d], dst_ref=rbuf.at[stage, d],
                send_sem=s_sem.at[stage, d], recv_sem=r_sem.at[stage, d],
                device_id=(w, to), device_id_type=MESH,
            )
            copy.start()
            return copy

        pending = []

        def send_strips(stage, east, north, mat, offs):
            res = permute(jnp.concatenate([east, north], axis=1), mat)
            copies = []
            for d in range(2):
                sbuf[stage, d] = res[:, d * 256 : (d + 1) * 256]
            for d in range(2):
                copies.append(send(stage, d, fwd(offs[d])))
            pending.extend(copies)
            return copies

        def received(copies, stage):
            for copy in copies:
                copy.wait_recv()
            return rbuf[stage, 0] + rbuf[stage, 1]

        def pack_into(dst, src, v, first, pad):
            g, u = v // 16, v % 16
            moved = roll(src[:, chunk(v + pad)], 4 * u - first)
            take = ((l64 >> 2) == u) & ((l64 & 3) < 3)
            here = pl.ds(g * LANES, LANES)
            dst[:, here] = jnp.where(take, moved, dst[:, here])

        def pack_group(src, g, first, pad, us, start):
            acc = start
            for u in us:
                moved = roll(src[:, chunk(16 * g + u + pad)], 4 * u - first)
                acc = jnp.where(((l64 >> 2) == u) & ((l64 & 3) < 3), moved, acc)
            return acc

        def pack(dst, src, first, pad):
            for g in range(2):
                dst[:, pl.ds(g * LANES, LANES)] = pack_group(src, g, first, pad, range(16), jnp.zeros((rows, LANES), F32))

        build(wx, 0, off_x, 0, False)
        q[pl.ds(levels, rows - levels), :] = jnp.zeros((rows - levels, CELLS), F32)
        loads[0].wait()

        @pl.loop(0, NV)
        def _(v):
            q[pl.ds(0, levels), chunk(v)] = qi[pl.ds(v, levels, stride=NV), :]

        pack(epack, q, 61, 0)
        strips = permute(jnp.concatenate([epack[...], q[:, pl.ds(CELLS - 256, 256)]], axis=1), wx)
        for d in range(2):
            sbuf[0, d] = strips[:, d * 256 : (d + 1) * 256]
        pl.semaphore_wait(barrier, len(partners))
        first = [send(0, d, fwd(off_x[d])) for d in range(2)]
        pending.extend(first)

        loads[1].wait()
        loads[2].wait()
        for c, cb in ((cx, cxb), (cy, cyb)):
            c[pl.ds(levels, rows - levels), :] = jnp.zeros((rows - levels, CELLS), F32)

            @pl.loop(0, NV)
            def _(v, c=c, cb=cb):
                c[pl.ds(0, levels), chunk(v)] = cb[:, chunk(v)].astype(F32)

        def x_interior():
            @pl.loop(0, NV)
            def _(v):
                here = q[:, chunk(v)]
                a1, a2, a3 = coefs(cx[:, chunk(v)])
                r1, r2, r3 = roll(here, 1), roll(here, 2), roll(here, 3)
                flux = (
                    jnp.where(l64 >= 1, r1, 0.0) * a1
                    + jnp.where(l64 >= 2, r2, 0.0) * a2
                    + jnp.where(l64 >= 3, r3, 0.0) * a3
                )
                outlet = here * a1 + r1 * a2 + r2 * a3
                bx[:, chunk(v + 2)] = here + flux - jnp.where(l64 == SIDE - 1, outlet, roll(flux, -1))

        x_interior()

        for i in range(3):
            loads[5 + i].wait()
            x = sq[i]
            sq2[i, :, pl.ds(0, SIDE)] = x

        for i in range(3):
            x = sq2[i]
            sq2[i] = jnp.where(lanes_of((SIDE, LANES)) < SIDE, x, pltpu.roll(x, SIDE, 1))

        for i in range(3):
            @pl.loop(0, NV)
            def _(v, i=i):
                row = jnp.where(low1, sq2[i, pl.ds(2 * v, 1), :], sq2[i, pl.ds(2 * v + 1, 1), :])
                flat[i, :, chunk(v)] = jnp.broadcast_to(row, (8, LANES))

        loads[3].wait()
        loads[4].wait()
        diag = lax.broadcasted_iota(I32, (levels, levels), 0) == lax.broadcasted_iota(I32, (levels, levels), 1)
        for i, col in ((0, kcol), (1, pcol)):
            column = jnp.sum(jnp.where(diag, jnp.broadcast_to(kp[i], (levels, levels)), 0.0), axis=1, keepdims=True)
            col[...] = jnp.zeros((rows, LANES), F32)
            col[pl.ds(0, levels), :] = jnp.broadcast_to(column, (levels, LANES))
        inv = 1.0 / jnp.sum(kp[0], axis=1, keepdims=True)
        inv8 = jnp.broadcast_to(inv, (8, LANES))

        sset[pl.ds(0, rows), :] = cy[:, pl.ds(0, 256)]
        for i in range(2):
            sset[pl.ds(rows + 8 * i, 8), :] = flat[1 + i, :, pl.ds(0, 256)]
        sets = []
        for d in range(2):
            copy = pltpu.make_async_remote_copy(
                src_ref=sset, dst_ref=rset.at[d], send_sem=sset_sem.at[d], recv_sem=rset_sem.at[d],
                device_id=(w, bwd(off_y[d])), device_id_type=MESH,
            )
            copy.start()
            sets.append(copy)

        build(wy, 3, off_y, 1, False)

        pack(cpack, cx, 0, 0)
        part = lanes_of((rows, 256)) & 3
        p1, p2, p3 = coefs(cpack[...])
        west1 = jnp.where(part == 0, p1, 0.0)
        west2 = jnp.where(part <= 1, p2, 0.0)
        west3 = jnp.where(part <= 2, p3, 0.0)
        cpack3 = (west1, west2, west3)

        def roll2(x, shift):
            return jnp.concatenate([roll(x[:, :LANES], shift), roll(x[:, LANES:], shift)], axis=1)

        def west_change(panel):
            f = panel * cpack3[2] + roll2(panel, -1) * cpack3[1] + roll2(panel, -2) * cpack3[0]
            return jnp.where(part < 3, f - roll2(f, -1), 0.0)

        def unpacked(src, g, u, first, mask):
            return jnp.where(mask, roll(src[:, g * LANES : (g + 1) * LANES], first - 4 * u), 0.0)

        def add_west(v):
            bx[:, chunk(v + 2)] = bx[:, chunk(v + 2)] + unpacked(dbuf, v // 16, v % 16, 0, l64 < 3)

        def y_flux(qv_r, q1, q1_r, q2_r, c):
            a1, a2, a3 = coefs(c)
            s1 = jnp.where(low, q1_r, qv_r)
            return s1 * a1 + q1 * a2 + jnp.where(low, q2_r, q1_r) * a3

        def y_start():
            q31, q30 = bx[:, chunk(NV + 1)], bx[:, chunk(NV)]
            r31, r30 = roll(q31, SIDE), roll(q30, SIDE)
            a1, a2, a3 = coefs(cy[:, chunk(NV - 1)])
            outlet = q31 * a1 + jnp.where(low, r30, r31) * a2 + q30 * a3
            return q31, r31, q30, r30, outlet

        def y_step(v, carry):
            qv, rv, q1, r1, above = carry
            q2 = bx[:, chunk(v)]
            r2 = roll(q2, SIDE)
            flux = y_flux(rv, q1, r1, r2, cy[:, chunk(v)])
            turned = roll(flux, SIDE)
            return qv + flux - jnp.where(low, turned, above), (q1, r1, q2, r2, turned)

        def emitted(v):
            return pcol[...] * jnp.concatenate([flat[0, :, chunk(v)]] * (rows // 8), axis=0)

        def sum_levels(x, col):
            x = x * col
            acc = x[0:8]
            for i in range(1, rows // 8):
                acc = acc + x[8 * i : 8 * i + 8]
            return acc

        def down(x):
            return jnp.broadcast_to(jnp.sum(x, axis=0, keepdims=True), (8, LANES))

        def tall(x):
            return jnp.concatenate([x] * (rows // 8), axis=0)

        pack(epack, bx, 61, 2)
        panel = received(first, 0)
        dbuf[...] = west_change(panel)
        add_west(NV - 2)
        add_west(NV - 1)
        y1 = send_strips(1, epack[...], bx[:, pl.ds(CELLS, 256)], wy, off_y)
        for v in range(NV - 2):
            add_west(v)

        def forward(v, carry):
            res, carry = y_step(v, carry)
            q[:, chunk(v)] = res + emitted(v)
            return carry

        carry = lax.fori_loop(0, NV - 2, lambda i, carry: forward(NV - 1 - i, carry), y_start())
        epack[:, pl.ds(0, LANES)] = pack_group(q, 0, 61, 0, range(2, 16), jnp.zeros((rows, LANES), F32))
        epack[:, pl.ds(LANES, LANES)] = pack_group(q, 1, 61, 0, range(16), jnp.zeros((rows, LANES), F32))

        bx[:, pl.ds(0, 256)] = received(y1, 1)
        for v in (1, 0):
            carry = forward(v, carry)
        epack[:, pl.ds(0, LANES)] = pack_group(q, 0, 61, 0, range(2), epack[:, pl.ds(0, LANES)])

        x2 = send_strips(2, epack[...], q[:, pl.ds(CELLS - 256, 256)], wx, off_x)
        x_interior()
        pack(epack, bx, 61, 2)
        build(wyt, 3, off_y, 1, True)
        for copy in sets:
            copy.wait_recv()

        panel = received(x2, 2)
        dbuf[...] = west_change(panel)
        add_west(NV - 2)
        add_west(NV - 1)
        y2 = send_strips(3, epack[...], bx[:, pl.ds(CELLS, 256)], wy, off_y)
        for v in range(NV - 2):
            add_west(v)

        def misfit_weight(col, v_obs, v_pre):
            return v_pre * (col * inv8 - v_obs) * inv8

        k_all = kcol[...]
        zero = jnp.zeros((rows, LANES), F32)
        q0_, q1_, q2_ = bx[:, chunk(2)], bx[:, chunk(3)], bx[:, chunk(4)]
        t0, t1, t2 = roll(q0_, SIDE), roll(q1_, SIDE), roll(q2_, SIDE)
        above = roll(y_flux(t2, q1_, t1, t0, cy[:, chunk(2)]), SIDE)
        f1 = y_flux(t1, q0_, t0, zero, cy[:, chunk(1)])
        f0 = y_flux(t0, zero, zero, zero, cy[:, chunk(0)])
        g1, g0 = roll(f1, SIDE), roll(f0, SIDE)
        n1 = q1_ + f1 - jnp.where(low, g1, above) + emitted(1)
        n0 = q0_ + f0 - jnp.where(low, g0, g1) + emitted(0)
        for v, n in ((0, n0), (1, n1)):
            scol[:, chunk(v)] = down(sum_levels(n, k_all))
        cols = []
        for d in range(2):
            copy = pltpu.make_async_remote_copy(
                src_ref=scol, dst_ref=rcol.at[d], send_sem=scol_sem.at[d], recv_sem=rcol_sem.at[d],
                device_id=(w, bwd(off_y[d])), device_id_type=MESH,
            )
            copy.start()
            cols.append(copy)

        def last(v, carry):
            res, carry = y_step(v, carry)
            col = down(sum_levels(res + emitted(v), k_all))
            gf[:, chunk(v)] = misfit_weight(col, flat[1, :, chunk(v)], flat[2, :, chunk(v)])
            return carry

        carry = lax.fori_loop(0, NV - 2, lambda i, carry: last(NV - 1 - i, carry), y_start())

        def terms(v, below):
            here = gf[:, chunk(v)]
            diff = here - jnp.where(low8, roll(below, SIDE), roll(here, SIDE))
            bar = k_all * tall(diff)
            a1, a2, a3 = coefs(cy[:, chunk(v)])
            return bar * a1, bar * a2, bar * a3

        def up_step(v, made, carry):
            first_above, second_above, third_above, third_above2 = carry
            m1, m2, m3 = made
            turned1, turned3 = roll(m1, SIDE), roll(m3, SIDE)
            res = (
                k_all * tall(gf[:, chunk(v)])
                + jnp.where(low, turned1, first_above)
                + second_above
                + jnp.where(low, third_above, third_above2)
            )
            mu[:, chunk(v)] = res
            return turned1, m2, turned3, third_above

        gf[:, chunk(0)] = jnp.zeros((8, LANES), F32)
        gf[:, chunk(1)] = jnp.zeros((8, LANES), F32)
        top = -k_all * tall(roll(gf[:, chunk(NV - 1)], SIDE))
        b1, b2, b3 = coefs(roll(cy[:, chunk(NV - 1)], SIDE))
        e1 = jnp.where(low, top * b1, 0.0)
        e2 = jnp.where(low, top * b2, 0.0)
        e3 = jnp.where(low, top * b3, 0.0)
        start = (roll(e1, SIDE), e2, roll(e3, SIDE), zero)

        def climb(i, state):
            v = NV - 1 - i
            made = terms(v, gf[:, chunk(v - 1)])
            return up_step(v, made, state)

        state3 = lax.fori_loop(0, NV - 3, climb, start)
        state2 = up_step(2, terms(2, gf[:, chunk(1)]), state3)

        dbuf[:, pl.ds(0, LANES)] = pack_group(mu, 0, 0, 0, range(2, 16), zero)
        dbuf[:, pl.ds(LANES, LANES)] = pack_group(mu, 1, 0, 0, range(14), zero)
        build(wxt, 0, off_x, 0, True)

        bars = []
        for d in range(2):
            cols[d].wait_recv()
            pa, pb = sbuf[3, d, :, pl.ds(0, LANES)], sbuf[3, d, :, pl.ds(LANES, LANES)]
            ra, rb = roll(pa, SIDE), roll(pb, SIDE)
            c0, c1 = rset[d, pl.ds(0, rows), pl.ds(0, LANES)], rset[d, pl.ds(0, rows), pl.ds(LANES, LANES)]
            z1, z2, z3 = coefs(c0)
            o1, o2, o3 = coefs(c1)
            h0 = jnp.where(low, rb, 0.0) * z1 + pb * z2 + jnp.where(low, ra, rb) * z3
            h1 = jnp.where(low, rb, 0.0) * o3
            k0, k1 = roll(h0, SIDE), roll(h1, SIDE)
            d0 = h0 - jnp.where(low, k0, k1)
            d1 = h1 - jnp.where(low, k1, 0.0)
            w0 = misfit_weight(
                rcol[d, :, chunk(0)] + down(sum_levels(d0, k_all)),
                rset[d, pl.ds(rows, 8), chunk(0)], rset[d, pl.ds(rows + 8, 8), chunk(0)],
            )
            w1 = misfit_weight(
                rcol[d, :, chunk(1)] + down(sum_levels(d1, k_all)),
                rset[d, pl.ds(rows, 8), chunk(1)], rset[d, pl.ds(rows + 8, 8), chunk(1)],
            )
            turned = roll(w0, SIDE)
            bar0 = k_all * tall(w0 - jnp.where(low8, 0.0, turned))
            bar1 = k_all * tall(w1 - jnp.where(low8, turned, roll(w1, SIDE)))
            third0, third1 = roll(bar0 * z3, SIDE), roll(bar1 * o3, SIDE)
            near_rows = jnp.where(low, 0.0, roll(bar0 * z1, SIDE)) + bar0 * z2 + jnp.where(low, third0, third1)
            far_rows = jnp.where(low, 0.0, third0)
            bars.append(jnp.concatenate([far_rows, near_rows], axis=1))
        back = permute(jnp.concatenate(bars, axis=1), wyt)
        back_east, back_north = back[:, :256], back[:, 256:]

        bx[:, pl.ds(0, 256)] = received(y2, 3)
        for v in (1, 0):
            carry = last(v, carry)
        state = up_step(2, terms(2, gf[:, chunk(1)]), state3)
        state = up_step(1, terms(1, gf[:, chunk(0)]), state)
        state = up_step(0, terms(0, jnp.zeros((8, LANES), F32)), state)
        mu[:, pl.ds(CELLS - 256, 256)] = mu[:, pl.ds(CELLS - 256, 256)] + back_north
        west0 = pack_group(mu, 0, 0, 0, range(2), dbuf[:, pl.ds(0, LANES)])
        west1_ = pack_group(mu, 1, 0, 0, range(14, 16), dbuf[:, pl.ds(LANES, LANES)])
        west = jnp.concatenate([west0, west1_], axis=1)
        diff = west - jnp.where(part > 0, roll2(west, 1), 0.0)
        pbar = diff * cpack3[2] + roll2(diff * cpack3[1], 1) + roll2(diff * cpack3[0], 2)
        p_all = pcol[...]
        for v in range(2):
            spb[:, chunk(v)] = down(sum_levels(pbar[:, v * LANES : (v + 1) * LANES], p_all))
        finals = []
        for r in range(windows):
            for d in range(2):
                copy = pltpu.make_async_remote_copy(
                    src_ref=spb, dst_ref=rpb.at[d, r], send_sem=spb_sem.at[d, r], recv_sem=rpb_sem.at[d, r],
                    device_id=(win_of(r), bwd(off_x[d])), device_id_type=MESH,
                )
                copy.start()
                finals.append(copy)

        for v in range(NV):
            mu[:, chunk(v)] = mu[:, chunk(v)] + unpacked(back_east, v // 16, v % 16, 61, l64 >= 61)
        both = jnp.broadcast_to(jnp.sum(kcol[...] * pcol[...], axis=0, keepdims=True), (8, LANES))

        @pl.loop(0, NV)
        def _(v):
            m = mu[:, chunk(v)] * p_all
            a1, a2, a3 = coefs(cx[:, chunk(v)])
            f = m - jnp.where(l64 >= 1, roll(m, 1), 0.0)
            ones = jnp.ones((rows, LANES), F32)
            s0 = sum_levels(m, ones)
            s1, s2, s3 = sum_levels(f * a1, ones), sum_levels(f * a2, ones), sum_levels(f * a3, ones)
            z1, z2, z3 = sum_levels(m * a1, ones), sum_levels(m * a2, ones), sum_levels(m * a3, ones)
            res = s0 + jnp.where(l64_8 < 63, roll(s1, -1), -z1)
            res = res + jnp.where(l64_8 < 62, roll(s2, -2), jnp.where(l64_8 == 62, -roll(z2, -1), 0.0))
            res = res + jnp.where(l64_8 < 61, roll(s3, -3), jnp.where(l64_8 == 61, -roll(z3, -2), 0.0))
            gint[pl.ds(v, 1), :] = (down(res) + both * gf[:, chunk(v)])[0:1]

        sums = []
        for r in range(1, windows):
            to = win_of(r)
            copy = pltpu.make_async_remote_copy(
                src_ref=gint.at[pl.ds(pl.multiple_of(to * per, per), per), :], dst_ref=rg.at[r - 1],
                send_sem=sg_sem.at[r - 1], recv_sem=rg_sem.at[r - 1],
                device_id=(to, t), device_id_type=MESH,
            )
            copy.start()
            sums.append(copy)

        for copy in finals:
            copy.wait_recv()
        halves = []
        for d in range(2):
            acc = rpb[d, 0]
            for r in range(1, windows):
                acc = acc + rpb[d, r]
            halves.append(acc)
        ends = permute(jnp.concatenate(halves, axis=1), wxt)
        for v in range(NV):
            g, u = v // 16, v % 16
            row = jnp.where(l64_8 >= 61, roll(ends[:, g * LANES : (g + 1) * LANES], 61 - 4 * u), 0.0)
            if v >= NV - 2:
                at = 256 + (v - NV + 2) * LANES
                row = row + ends[:, at : at + LANES]
            fin[pl.ds(v, 1), :] = row[0:1]
        mine = pl.ds(pl.multiple_of(w * per, per), per)
        total = gint[mine, :] + fin[mine, :]
        for copy in sums:
            copy.wait_recv()
        for r in range(1, windows):
            total = total + rg[r - 1]
        out[0, pl.ds(0, per, stride=2), :] = total[:, :SIDE]
        out[0, pl.ds(1, per, stride=2), :] = pltpu.roll(total, SIDE, 1)[:, :SIDE]

        for copy in pending + sets + cols + finals + sums:
            copy.wait_send()

    return kernel, rows, per


def body(initial, courant_x, courant_y, observed, precision_w, kernel, profile, emission, edges):
    levels = initial.shape[2]
    windows = lax.axis_size("win")
    run, rows, per = make_kernel(levels, windows)
    vm = pltpu.VMEM
    dma = pltpu.SemaphoreType.DMA
    anywhere = pl.BlockSpec(memory_space=pl.ANY)
    return pl.pallas_call(
        run,
        out_shape=jax.ShapeDtypeStruct((1, 2 * per, SIDE), F32),
        in_specs=[anywhere] * 8 + [pl.BlockSpec(memory_space=pltpu.SMEM)],
        out_specs=pl.BlockSpec(memory_space=pltpu.VMEM),
        scratch_shapes=[
            vm((levels * NV, LANES), F32),
            vm((rows, CELLS), F32),
            vm((rows, CELLS + 256), F32),
            vm((rows, CELLS), F32),
            vm((rows, CELLS), F32),
            vm((rows, CELLS), F32),
            vm((levels, CELLS), BF16),
            vm((levels, CELLS), BF16),
            vm((3, SIDE, SIDE), F32),
            vm((3, SIDE, LANES), F32),
            vm((3, 8, CELLS), F32),
            vm((2, 1, levels), F32),
            vm((rows, LANES), F32),
            vm((rows, LANES), F32),
            vm((8, CELLS), F32),
            vm((512, 512), BF16),
            vm((512, 512), BF16),
            vm((512, 512), BF16),
            vm((512, 512), BF16),
            vm((rows, 256), F32),
            vm((rows, 256), F32),
            vm((rows, 256), F32),
            vm((4, 2, rows, 256), F32),
            vm((4, 2, rows, 256), F32),
            vm((rows + 16, 256), F32),
            vm((2, rows + 16, 256), F32),
            vm((8, 256), F32),
            vm((2, 8, 256), F32),
            vm((8, 256), F32),
            vm((2, windows, 8, 256), F32),
            vm((NV, LANES), F32),
            vm((windows - 1, per, LANES), F32),
            vm((NV, LANES), F32),
            dma((8,)),
            dma((4, 2)),
            dma((4, 2)),
            dma((2,)),
            dma((2,)),
            dma((2,)),
            dma((2,)),
            dma((2, windows)),
            dma((2, windows)),
            dma((windows - 1,)),
            dma((windows - 1,)),
        ],
        compiler_params=pltpu.CompilerParams(collective_id=0, has_side_effects=True),
    )(
        initial.reshape(levels * NV, LANES), courant_x, courant_y, observed, precision_w,
        kernel.reshape(1, levels), profile.reshape(1, levels), emission, edges,
    )


def solution(mesh):
    placed = (
        P("win", "tile", None, None),
        P("win", "tile", None, None),
        P("win", "tile", None, None),
        P("win", "tile", None, None),
        P("win", "tile", None, None),
        P(),
        P(),
        P("tile", None, None),
        P(),
    )
    return jax.shard_map(
        body, mesh=mesh, in_specs=placed, out_specs=P("tile", "win", None), check_vma=False
    )
```

time: 284 us -> 52.8 us (0.19); the launches traced: 279 us -> 52.6 us
  local copies, waits for them, and re-layouts: 146 us -> 1.3 us
  other arithmetic: 74.5 us -> 0 us
  Pallas kernels: 0 us -> 51.3 us
  waiting for transfers between devices: 22.9 us -> 0 us
  starting transfers between devices: 15.6 us -> 0 us
  blocking collectives: 15.2 us -> 0 us
  between operations: 4.62 us -> 0.01 us
    pallas_call x0 -> x1, Pallas kernels: none -> 51.3 us  [body(): pl.pallas_call(run, out_shape=jax.ShapeDtypeStruct((1, 2 * per, SIDE), F3...]
    scatter-add x4 -> x0, local copies, waits for them, and re-layouts: 37.5 us -> none  [the longest x2 19.5 us: add_strips(): tracer_field_adjoint.at[..., side_len - 3:, :].add(north_bar[..., ::-1, :])]
    rev x14 -> x0, local copies, waits for them, and re-layouts: 25.2 us -> none  [the longest x2 6.64 us: as_halo(): return jnp.swapaxes(panel[..., ::-1, :], -1, -2)]
    add x13 -> x0, other arithmetic: 24.1 us -> none  [the longest x2 7.73 us: advect_along(): inflow + lax.slice_in_dim(extended, 3 - depth, 3 - depth + side_len, axis...]
    ppermute x12 -> x0, waiting for transfers between devices: 22.9 us -> none  [from_behind(): return lax.ppermute(block, axis, route)]
    unnamed x67 -> x1, local copies, waits for them, and re-layouts: 20.8 us -> 1.3 us
    ppermute x12 -> x0, starting transfers between devices: 15.6 us -> none  [from_behind(): return lax.ppermute(block, axis, route)]
    psum x1 -> x0, blocking collectives: 15.2 us -> none  [body(): summed_all = lax.psum(gradient, 'win')]
  transfers between devices with their start and end apart: 12 -> 0, of which waited for: 6 -> 0; matrix products, arithmetic and copies ran while one was open for 11% -> 0% of each run, Pallas kernels for 0% -> 0%
where the time goes in v1:
time: 52.8 us; the launch traced here: 52.6 us
  Pallas kernels  51.3 us (97%)
  local copies, waits for them, and re-layouts  1.3 us (2%)
    pallas_call x1, Pallas kernels, body(): pl.pallas_call(run, out_shape=jax.ShapeDtypeStruct((1, 2 * per, SIDE), F3...  51.3 us
    unnamed x1, local copies, waits for them, and re-layouts  1.3 us

profile of v1, /device:TPU:1, one launch (start us, length us, event | category | flops | bytes accessed | tf_op | source)
XLA Modules:
  0.0 52.6 jit_solution(6948395249851530541)
XLA Ops:
  0.0 51.3 %shard_map.91 = f32[1,16,64]{2,1,0:T(8,128)} custom-call(f32[1152,128]{1,0:T(8,128)} %bitcast.3, bf16[1,1,36,4096]{3,2,1,0:T(8,128)(2,1)} %cx_h.1, bf16[1,1,36,4096]{3,2,1,0:T(8,128)(2,1)} %cy_h.1, f32[1,1,64,64]{3,2,1,0:T(8,128)} %obs_h.1, f32[1,1,64,64]{3,2,1,0:T(8,128)} %pre_h.1, f32[1,36]{1,0:T(1,128)} %bitcast.4, f32[1,36]{1,0:T(1,128)} %bitcast.5, ...), custom_call_target="tpu_custom_call" | custom-call | tf_op jit(solution)/shard_map/pallas_call | solution.py:566
  51.3 1.3 %copy.11 = f32[1,16,64]{2,1,0:T(8,128)} copy(f32[1,16,64]{2,1,0:T(8,128)} %shard_map.91) | data formatting | bytes 8192

commit v2 on v1

--- a/solution.py
+++ b/solution.py
@@ -24,7 +24,8 @@
 
 
 def coefs(c):
-    return jnp.clip(c, 0.0, 1.0), jnp.clip(c - 1.0, 0.0, 1.0), jnp.clip(c - 2.0, 0.0, 1.0)
+    one, three = jnp.minimum(c, 1.0), jnp.maximum(c - 2.0, 0.0)
+    return one, c - one - three, three
 
 
 def chunk(v):
@@ -50,8 +51,8 @@
     def kernel(
         init_h, cx_h, cy_h, obs_h, pre_h, ker_h, pro_h, emi_h, edges,
         out,
-        qi, q, bx, mu, cx, cy, cxb, cyb, sq, sq2, flat, kp, kcol, pcol, gf,
-        wx, wxt, wy, wyt, epack, cpack, dbuf,
+        qi, q, bx, mu, cx, cy, cxb, cyb, sq, sq2, flat, kp, kcol, pcol, gf, df, bfix,
+        wx, wxt, wy, wyt, epack, ewrap, cpack, dbuf,
         sbuf, rbuf, sset, rset, scol, rcol, spb, rpb, gint, rg, fin,
         in_sem, s_sem, r_sem, sset_sem, rset_sem, scol_sem, rcol_sem, spb_sem, rpb_sem, sg_sem, rg_sem,
     ):
@@ -71,16 +72,20 @@
             return lax.rem(w + r, windows)
 
         loads = [
-            pltpu.make_async_copy(init_h, qi, in_sem.at[0]),
-            pltpu.make_async_copy(cx_h.at[0, 0], cxb, in_sem.at[1]),
-            pltpu.make_async_copy(cy_h.at[0, 0], cyb, in_sem.at[2]),
-            pltpu.make_async_copy(ker_h, kp.at[0], in_sem.at[3]),
-            pltpu.make_async_copy(pro_h, kp.at[1], in_sem.at[4]),
-            pltpu.make_async_copy(emi_h.at[0], sq.at[0], in_sem.at[5]),
-            pltpu.make_async_copy(obs_h.at[0, 0], sq.at[1], in_sem.at[6]),
-            pltpu.make_async_copy(pre_h.at[0, 0], sq.at[2], in_sem.at[7]),
+            pltpu.make_async_copy(cx_h.at[0, 0], cxb, in_sem.at[0]),
+            pltpu.make_async_copy(cy_h.at[0, 0], cyb, in_sem.at[1]),
+            pltpu.make_async_copy(ker_h, kp.at[0], in_sem.at[2]),
+            pltpu.make_async_copy(pro_h, kp.at[1], in_sem.at[3]),
+            pltpu.make_async_copy(emi_h.at[0], sq.at[0], in_sem.at[4]),
+            pltpu.make_async_copy(obs_h.at[0, 0], sq.at[1], in_sem.at[5]),
+            pltpu.make_async_copy(pre_h.at[0, 0], sq.at[2], in_sem.at[6]),
         ]
-        for load in loads:
+        tiles_of = rows // 8
+        fields = []
+        for i in range(tiles_of):
+            some = pl.ds(8 * NV * i, NV * min(8, levels - 8 * i))
+            fields.append(pltpu.make_async_copy(init_h.at[some, :], qi.at[some, :], in_sem.at[7 + i]))
+        for load in fields + loads:
             load.start()
 
         barrier = pltpu.get_barrier_semaphore()
@@ -174,12 +179,18 @@
                 copy.wait_recv()
             return rbuf[stage, 0] + rbuf[stage, 1]
 
-        def pack_into(dst, src, v, first, pad):
-            g, u = v // 16, v % 16
-            moved = roll(src[:, chunk(v + pad)], 4 * u - first)
-            take = ((l64 >> 2) == u) & ((l64 & 3) < 3)
-            here = pl.ds(g * LANES, LANES)
-            dst[:, here] = jnp.where(take, moved, dst[:, here])
+        def roll2(x, shift):
+            return jnp.concatenate([roll(x[:, :LANES], shift), roll(x[:, LANES:], shift)], axis=1)
+
+        slot8 = jnp.where((l64_8 & 3) < 3, l64_8 >> 2, -1)
+
+        def put(acc, x, v, first):
+            return jnp.where(slot8 == v % 16, roll(x, 4 * (v % 16) - first), acc)
+
+        def tile_rows(i):
+            if isinstance(i, int):
+                return pl.ds(8 * i, 8)
+            return pl.ds(pl.multiple_of(8 * i, 8), 8)
 
         def pack_group(src, g, first, pad, us, start):
             acc = start
@@ -193,14 +204,18 @@
                 dst[:, pl.ds(g * LANES, LANES)] = pack_group(src, g, first, pad, range(16), jnp.zeros((rows, LANES), F32))
 
         build(wx, 0, off_x, 0, False)
-        q[pl.ds(levels, rows - levels), :] = jnp.zeros((rows - levels, CELLS), F32)
-        loads[0].wait()
-
-        @pl.loop(0, NV)
-        def _(v):
-            q[pl.ds(0, levels), chunk(v)] = qi[pl.ds(v, levels, stride=NV), :]
-
-        pack(epack, q, 61, 0)
+        if levels < rows:
+            qi[pl.ds(levels * NV, (rows - levels) * NV), :] = jnp.zeros(((rows - levels) * NV, LANES), F32)
+        for i in range(tiles_of):
+            fields[i].wait()
+            acc = [jnp.zeros((8, LANES), F32)] * 2
+            for v in range(NV):
+                here = qi[pl.ds(8 * NV * i + v, 8, stride=NV), :]
+                q[tile_rows(i), chunk(v)] = here
+                acc[v // 16] = put(acc[v // 16], here, v, 61)
+            epack[tile_rows(i), pl.ds(0, LANES)] = acc[0]
+            epack[tile_rows(i), pl.ds(LANES, LANES)] = acc[1]
+
         strips = permute(jnp.concatenate([epack[...], q[:, pl.ds(CELLS - 256, 256)]], axis=1), wx)
         for d in range(2):
             sbuf[0, d] = strips[:, d * 256 : (d + 1) * 256]
@@ -208,33 +223,38 @@
         first = [send(0, d, fwd(off_x[d])) for d in range(2)]
         pending.extend(first)
 
+        loads[0].wait()
         loads[1].wait()
-        loads[2].wait()
         for c, cb in ((cx, cxb), (cy, cyb)):
             c[pl.ds(levels, rows - levels), :] = jnp.zeros((rows - levels, CELLS), F32)
 
-            @pl.loop(0, NV)
+            @pl.loop(0, NV // 8)
             def _(v, c=c, cb=cb):
-                c[pl.ds(0, levels), chunk(v)] = cb[:, chunk(v)].astype(F32)
+                some = pl.ds(pl.multiple_of(v * 8 * LANES, 8 * LANES), 8 * LANES)
+                c[pl.ds(0, levels), some] = cb[:, some].astype(F32)
 
         def x_interior():
-            @pl.loop(0, NV)
-            def _(v):
-                here = q[:, chunk(v)]
-                a1, a2, a3 = coefs(cx[:, chunk(v)])
-                r1, r2, r3 = roll(here, 1), roll(here, 2), roll(here, 3)
-                flux = (
-                    jnp.where(l64 >= 1, r1, 0.0) * a1
-                    + jnp.where(l64 >= 2, r2, 0.0) * a2
-                    + jnp.where(l64 >= 3, r3, 0.0) * a3
-                )
-                outlet = here * a1 + r1 * a2 + r2 * a3
-                bx[:, chunk(v + 2)] = here + flux - jnp.where(l64 == SIDE - 1, outlet, roll(flux, -1))
+            @pl.loop(0, tiles_of)
+            def _(i):
+                here_rows = tile_rows(i)
+                ewrap[here_rows, :] = roll2(epack[here_rows, :], SIDE)
+                acc = [jnp.zeros((8, LANES), F32)] * 2
+                for v in range(NV):
+                    here = q[here_rows, chunk(v)]
+                    a1, a2, a3 = coefs(cx[here_rows, chunk(v)])
+                    r1, r2, r3 = roll(here, 1), roll(here, 2), roll(here, 3)
+                    flux = r1 * a1 + r2 * a2 + r3 * a3
+                    outlet = here * a1 + r1 * a2 + r2 * a3
+                    res = here + flux - jnp.where(l64_8 == SIDE - 1, outlet, roll(flux, -1))
+                    bx[here_rows, chunk(v + 2)] = res
+                    acc[v // 16] = put(acc[v // 16], res, v, 61)
+                epack[here_rows, pl.ds(0, LANES)] = acc[0]
+                epack[here_rows, pl.ds(LANES, LANES)] = acc[1]
 
         x_interior()
 
         for i in range(3):
-            loads[5 + i].wait()
+            loads[4 + i].wait()
             x = sq[i]
             sq2[i, :, pl.ds(0, SIDE)] = x
 
@@ -243,13 +263,15 @@
             sq2[i] = jnp.where(lanes_of((SIDE, LANES)) < SIDE, x, pltpu.roll(x, SIDE, 1))
 
         for i in range(3):
-            @pl.loop(0, NV)
-            def _(v, i=i):
-                row = jnp.where(low1, sq2[i, pl.ds(2 * v, 1), :], sq2[i, pl.ds(2 * v + 1, 1), :])
-                flat[i, :, chunk(v)] = jnp.broadcast_to(row, (8, LANES))
-
+            @pl.loop(0, NV // 8)
+            def _(k, i=i):
+                for j in range(8):
+                    v = k * 8 + j
+                    row = jnp.where(low1, sq2[i, pl.ds(2 * v, 1), :], sq2[i, pl.ds(2 * v + 1, 1), :])
+                    flat[i, :, chunk(v)] = jnp.broadcast_to(row, (8, LANES))
+
+        loads[2].wait()
         loads[3].wait()
-        loads[4].wait()
         diag = lax.broadcasted_iota(I32, (levels, levels), 0) == lax.broadcasted_iota(I32, (levels, levels), 1)
         for i, col in ((0, kcol), (1, pcol)):
             column = jnp.sum(jnp.where(diag, jnp.broadcast_to(kp[i], (levels, levels)), 0.0), axis=1, keepdims=True)
@@ -280,44 +302,55 @@
         west3 = jnp.where(part <= 2, p3, 0.0)
         cpack3 = (west1, west2, west3)
 
-        def roll2(x, shift):
-            return jnp.concatenate([roll(x[:, :LANES], shift), roll(x[:, LANES:], shift)], axis=1)
-
         def west_change(panel):
+            panel = panel - ewrap[...]
             f = panel * cpack3[2] + roll2(panel, -1) * cpack3[1] + roll2(panel, -2) * cpack3[0]
             return jnp.where(part < 3, f - roll2(f, -1), 0.0)
-
-        def unpacked(src, g, u, first, mask):
-            return jnp.where(mask, roll(src[:, g * LANES : (g + 1) * LANES], first - 4 * u), 0.0)
-
-        def add_west(v):
-            bx[:, chunk(v + 2)] = bx[:, chunk(v + 2)] + unpacked(dbuf, v // 16, v % 16, 0, l64 < 3)
 
         def y_flux(qv_r, q1, q1_r, q2_r, c):
             a1, a2, a3 = coefs(c)
             s1 = jnp.where(low, q1_r, qv_r)
             return s1 * a1 + q1 * a2 + jnp.where(low, q2_r, q1_r) * a3
 
-        def y_start():
-            q31, q30 = bx[:, chunk(NV + 1)], bx[:, chunk(NV)]
-            r31, r30 = roll(q31, SIDE), roll(q30, SIDE)
-            a1, a2, a3 = coefs(cy[:, chunk(NV - 1)])
-            outlet = q31 * a1 + jnp.where(low, r30, r31) * a2 + q30 * a3
-            return q31, r31, q30, r30, outlet
-
-        def y_step(v, carry):
-            qv, rv, q1, r1, above = carry
-            q2 = bx[:, chunk(v)]
-            r2 = roll(q2, SIDE)
-            flux = y_flux(rv, q1, r1, r2, cy[:, chunk(v)])
-            turned = roll(flux, SIDE)
-            return qv + flux - jnp.where(low, turned, above), (q1, r1, q2, r2, turned)
+        def y_interior(here_rows, finish, fixed=0):
+            changes = [dbuf[here_rows, pl.ds(g * LANES, LANES)] for g in range(2)]
+            xs, rs, turned, outlet = {}, {}, {}, None
+            done = {}
+            for v in range(NV):
+                xs[v] = bx[here_rows, chunk(v + 2)]
+                if v >= fixed:
+                    xs[v] = xs[v] + jnp.where(l64_8 < 3, roll(changes[v // 16], -4 * (v % 16)), 0.0)
+                if fixed <= v < 3:
+                    bx[here_rows, chunk(v + 2)] = xs[v]
+                rs[v] = roll(xs[v], SIDE)
+                if v < 2:
+                    continue
+                a1, a2, a3 = coefs(cy[here_rows, chunk(v)])
+                flux = jnp.where(low8, rs[v - 1], rs[v]) * a1 + xs[v - 1] * a2 + jnp.where(low8, rs[v - 2], rs[v - 1]) * a3
+                turned[v] = roll(flux, SIDE)
+                done[v] = xs[v] + flux
+                if v > 2:
+                    finish(v - 1, done[v - 1] - jnp.where(low8, turned[v - 1], turned[v]))
+                if v == NV - 1:
+                    outlet = xs[v] * a1 + jnp.where(low8, rs[v - 1], rs[v]) * a2 + xs[v - 1] * a3
+                    finish(v, done[v] - jnp.where(low8, turned[v], outlet))
+
+        def y_first(pa, pb):
+            q0_, q1_, q2_ = bx[:, chunk(2)], bx[:, chunk(3)], bx[:, chunk(4)]
+            t0, t1, t2 = roll(q0_, SIDE), roll(q1_, SIDE), roll(q2_, SIDE)
+            ta, tb = roll(pa, SIDE), roll(pb, SIDE)
+            above = roll(y_flux(t2, q1_, t1, t0, cy[:, chunk(2)]), SIDE)
+            f1 = y_flux(t1, q0_, t0, tb, cy[:, chunk(1)])
+            f0 = y_flux(t0, pb, tb, ta, cy[:, chunk(0)])
+            g1, g0 = roll(f1, SIDE), roll(f0, SIDE)
+            n1 = q1_ + f1 - jnp.where(low, g1, above) + emitted(1)
+            n0 = q0_ + f0 - jnp.where(low, g0, g1) + emitted(0)
+            return n0, n1
 
         def emitted(v):
             return pcol[...] * jnp.concatenate([flat[0, :, chunk(v)]] * (rows // 8), axis=0)
 
-        def sum_levels(x, col):
-            x = x * col
+        def sum_levels(x):
             acc = x[0:8]
             for i in range(1, rows // 8):
                 acc = acc + x[8 * i : 8 * i + 8]
@@ -329,59 +362,58 @@
         def tall(x):
             return jnp.concatenate([x] * (rows // 8), axis=0)
 
-        pack(epack, bx, 61, 2)
         panel = received(first, 0)
         dbuf[...] = west_change(panel)
-        add_west(NV - 2)
-        add_west(NV - 1)
-        y1 = send_strips(1, epack[...], bx[:, pl.ds(CELLS, 256)], wy, off_y)
-        for v in range(NV - 2):
-            add_west(v)
-
-        def forward(v, carry):
-            res, carry = y_step(v, carry)
-            q[:, chunk(v)] = res + emitted(v)
-            return carry
-
-        carry = lax.fori_loop(0, NV - 2, lambda i, carry: forward(NV - 1 - i, carry), y_start())
-        epack[:, pl.ds(0, LANES)] = pack_group(q, 0, 61, 0, range(2, 16), jnp.zeros((rows, LANES), F32))
-        epack[:, pl.ds(LANES, LANES)] = pack_group(q, 1, 61, 0, range(16), jnp.zeros((rows, LANES), F32))
-
-        bx[:, pl.ds(0, 256)] = received(y1, 1)
-        for v in (1, 0):
-            carry = forward(v, carry)
+        change = dbuf[:, pl.ds(LANES, LANES)]
+        ends_now = [
+            bx[:, chunk(v + 2)] + jnp.where(l64 < 3, roll(change, -4 * (v % 16)), 0.0) for v in (NV - 2, NV - 1)
+        ]
+        y1 = send_strips(1, epack[...], jnp.concatenate(ends_now, axis=1), wy, off_y)
+
+        @pl.loop(0, tiles_of)
+        def _(i):
+            here_rows = tile_rows(i)
+            acc = [jnp.zeros((8, LANES), F32)] * 2
+            share = pcol[here_rows, :]
+
+            def finish(v, res):
+                res = res + share * flat[0, :, chunk(v)]
+                q[here_rows, chunk(v)] = res
+                acc[v // 16] = put(acc[v // 16], res, v, 61)
+
+            y_interior(here_rows, finish)
+            epack[here_rows, pl.ds(0, LANES)] = acc[0]
+            epack[here_rows, pl.ds(LANES, LANES)] = acc[1]
+
+        panel = received(y1, 1)
+        for v, res in enumerate(y_first(panel[:, :LANES], panel[:, LANES:])):
+            q[:, chunk(v)] = res
         epack[:, pl.ds(0, LANES)] = pack_group(q, 0, 61, 0, range(2), epack[:, pl.ds(0, LANES)])
 
         x2 = send_strips(2, epack[...], q[:, pl.ds(CELLS - 256, 256)], wx, off_x)
         x_interior()
-        pack(epack, bx, 61, 2)
         build(wyt, 3, off_y, 1, True)
         for copy in sets:
             copy.wait_recv()
 
         panel = received(x2, 2)
         dbuf[...] = west_change(panel)
-        add_west(NV - 2)
-        add_west(NV - 1)
-        y2 = send_strips(3, epack[...], bx[:, pl.ds(CELLS, 256)], wy, off_y)
-        for v in range(NV - 2):
-            add_west(v)
+        change = dbuf[:, pl.ds(LANES, LANES)]
+        ends_now = [
+            bx[:, chunk(v + 2)] + jnp.where(l64 < 3, roll(change, -4 * (v % 16)), 0.0) for v in (NV - 2, NV - 1)
+        ]
+        y2 = send_strips(3, epack[...], jnp.concatenate(ends_now, axis=1), wy, off_y)
 
         def misfit_weight(col, v_obs, v_pre):
             return v_pre * (col * inv8 - v_obs) * inv8
 
         k_all = kcol[...]
         zero = jnp.zeros((rows, LANES), F32)
-        q0_, q1_, q2_ = bx[:, chunk(2)], bx[:, chunk(3)], bx[:, chunk(4)]
-        t0, t1, t2 = roll(q0_, SIDE), roll(q1_, SIDE), roll(q2_, SIDE)
-        above = roll(y_flux(t2, q1_, t1, t0, cy[:, chunk(2)]), SIDE)
-        f1 = y_flux(t1, q0_, t0, zero, cy[:, chunk(1)])
-        f0 = y_flux(t0, zero, zero, zero, cy[:, chunk(0)])
-        g1, g0 = roll(f1, SIDE), roll(f0, SIDE)
-        n1 = q1_ + f1 - jnp.where(low, g1, above) + emitted(1)
-        n0 = q0_ + f0 - jnp.where(low, g0, g1) + emitted(0)
-        for v, n in ((0, n0), (1, n1)):
-            scol[:, chunk(v)] = down(sum_levels(n, k_all))
+        change = dbuf[:, pl.ds(0, LANES)]
+        for v in range(3):
+            bx[:, chunk(v + 2)] = bx[:, chunk(v + 2)] + jnp.where(l64 < 3, roll(change, -4 * v), 0.0)
+        for v, n in enumerate(y_first(zero, zero)):
+            scol[:, chunk(v)] = down(sum_levels(n * k_all))
         cols = []
         for d in range(2):
             copy = pltpu.make_async_remote_copy(
@@ -391,53 +423,59 @@
             copy.start()
             cols.append(copy)
 
-        def last(v, carry):
-            res, carry = y_step(v, carry)
-            col = down(sum_levels(res + emitted(v), k_all))
+        gf[...] = jnp.zeros((8, CELLS), F32)
+
+        @pl.loop(0, tiles_of)
+        def _(i):
+            here_rows = tile_rows(i)
+            share, weight = pcol[here_rows, :], kcol[here_rows, :]
+
+            def finish(v, res):
+                gf[:, chunk(v)] = gf[:, chunk(v)] + (res + share * flat[0, :, chunk(v)]) * weight
+
+            y_interior(here_rows, finish, 3)
+
+        def weigh(v, col):
             gf[:, chunk(v)] = misfit_weight(col, flat[1, :, chunk(v)], flat[2, :, chunk(v)])
-            return carry
-
-        carry = lax.fori_loop(0, NV - 2, lambda i, carry: last(NV - 1 - i, carry), y_start())
-
-        def terms(v, below):
+
+        def slope(v):
             here = gf[:, chunk(v)]
-            diff = here - jnp.where(low8, roll(below, SIDE), roll(here, SIDE))
-            bar = k_all * tall(diff)
-            a1, a2, a3 = coefs(cy[:, chunk(v)])
-            return bar * a1, bar * a2, bar * a3
-
-        def up_step(v, made, carry):
-            first_above, second_above, third_above, third_above2 = carry
-            m1, m2, m3 = made
-            turned1, turned3 = roll(m1, SIDE), roll(m3, SIDE)
-            res = (
-                k_all * tall(gf[:, chunk(v)])
-                + jnp.where(low, turned1, first_above)
-                + second_above
-                + jnp.where(low, third_above, third_above2)
-            )
-            mu[:, chunk(v)] = res
-            return turned1, m2, turned3, third_above
-
-        gf[:, chunk(0)] = jnp.zeros((8, LANES), F32)
-        gf[:, chunk(1)] = jnp.zeros((8, LANES), F32)
-        top = -k_all * tall(roll(gf[:, chunk(NV - 1)], SIDE))
-        b1, b2, b3 = coefs(roll(cy[:, chunk(NV - 1)], SIDE))
-        e1 = jnp.where(low, top * b1, 0.0)
-        e2 = jnp.where(low, top * b2, 0.0)
-        e3 = jnp.where(low, top * b3, 0.0)
-        start = (roll(e1, SIDE), e2, roll(e3, SIDE), zero)
-
-        def climb(i, state):
-            v = NV - 1 - i
-            made = terms(v, gf[:, chunk(v - 1)])
-            return up_step(v, made, state)
-
-        state3 = lax.fori_loop(0, NV - 3, climb, start)
-        state2 = up_step(2, terms(2, gf[:, chunk(1)]), state3)
-
-        dbuf[:, pl.ds(0, LANES)] = pack_group(mu, 0, 0, 0, range(2, 16), zero)
-        dbuf[:, pl.ds(LANES, LANES)] = pack_group(mu, 1, 0, 0, range(14), zero)
+            before = roll(gf[:, chunk(v - 1)], SIDE) if v > 0 else jnp.zeros((8, LANES), F32)
+            return here - jnp.where(low8, before, roll(here, SIDE))
+
+        for v in range(2, NV):
+            weigh(v, down(gf[:, chunk(v)]))
+        for v in range(2, NV):
+            df[:, chunk(v)] = slope(v)
+
+        @pl.loop(0, tiles_of)
+        def _(i):
+            here_rows = tile_rows(i)
+            weight = kcol[here_rows, :]
+            none = jnp.zeros((8, LANES), F32)
+            top = -weight * roll(gf[:, chunk(NV - 1)], SIDE)
+            b1, b2, b3 = coefs(roll(cy[here_rows, chunk(NV - 1)], SIDE))
+            first_up = roll(jnp.where(low8, top * b1, 0.0), SIDE)
+            second_up = jnp.where(low8, top * b2, 0.0)
+            third_up, third_up2 = roll(jnp.where(low8, top * b3, 0.0), SIDE), none
+            acc = [none, none]
+            for v in range(NV - 1, 1, -1):
+                bar = weight * df[:, chunk(v)]
+                a1, a2, a3 = coefs(cy[here_rows, chunk(v)])
+                turned1, turned3 = roll(bar * a1, SIDE), roll(bar * a3, SIDE)
+                res = (
+                    weight * gf[:, chunk(v)]
+                    + jnp.where(low8, turned1, first_up)
+                    + second_up
+                    + jnp.where(low8, third_up, third_up2)
+                )
+                mu[here_rows, chunk(v)] = res
+                if v < NV - 2:
+                    acc[v // 16] = put(acc[v // 16], res, v, 0)
+                first_up, second_up, third_up, third_up2 = turned1, bar * a2, turned3, third_up
+            dbuf[here_rows, pl.ds(0, LANES)] = acc[0]
+            dbuf[here_rows, pl.ds(LANES, LANES)] = acc[1]
+
         build(wxt, 0, off_x, 0, True)
 
         bars = []
@@ -454,11 +492,11 @@
             d0 = h0 - jnp.where(low, k0, k1)
             d1 = h1 - jnp.where(low, k1, 0.0)
             w0 = misfit_weight(
-                rcol[d, :, chunk(0)] + down(sum_levels(d0, k_all)),
+                rcol[d, :, chunk(0)] + down(sum_levels(d0 * k_all)),
                 rset[d, pl.ds(rows, 8), chunk(0)], rset[d, pl.ds(rows + 8, 8), chunk(0)],
             )
             w1 = misfit_weight(
-                rcol[d, :, chunk(1)] + down(sum_levels(d1, k_all)),
+                rcol[d, :, chunk(1)] + down(sum_levels(d1 * k_all)),
                 rset[d, pl.ds(rows, 8), chunk(1)], rset[d, pl.ds(rows + 8, 8), chunk(1)],
             )
             turned = roll(w0, SIDE)
@@ -471,12 +509,21 @@
         back = permute(jnp.concatenate(bars, axis=1), wyt)
         back_east, back_north = back[:, :256], back[:, 256:]
 
-        bx[:, pl.ds(0, 256)] = received(y2, 3)
-        for v in (1, 0):
-            carry = last(v, carry)
-        state = up_step(2, terms(2, gf[:, chunk(1)]), state3)
-        state = up_step(1, terms(1, gf[:, chunk(0)]), state)
-        state = up_step(0, terms(0, jnp.zeros((8, LANES), F32)), state)
+        panel = received(y2, 3)
+        for v, n in enumerate(y_first(panel[:, :LANES], panel[:, LANES:])):
+            weigh(v, down(sum_levels(n * k_all)))
+        made = {}
+        for v in range(4):
+            bar = k_all * tall(slope(v))
+            a1, a2, a3 = coefs(cy[:, chunk(v)])
+            made[v] = (roll(bar * a1, SIDE), bar * a2, roll(bar * a3, SIDE))
+        for v in range(2):
+            mu[:, chunk(v)] = (
+                k_all * tall(gf[:, chunk(v)])
+                + jnp.where(low, made[v][0], made[v + 1][0])
+                + made[v + 1][1]
+                + jnp.where(low, made[v + 1][2], made[v + 2][2])
+            )
         mu[:, pl.ds(CELLS - 256, 256)] = mu[:, pl.ds(CELLS - 256, 256)] + back_north
         west0 = pack_group(mu, 0, 0, 0, range(2), dbuf[:, pl.ds(0, LANES)])
         west1_ = pack_group(mu, 1, 0, 0, range(14, 16), dbuf[:, pl.ds(LANES, LANES)])
@@ -485,7 +532,7 @@
         pbar = diff * cpack3[2] + roll2(diff * cpack3[1], 1) + roll2(diff * cpack3[0], 2)
         p_all = pcol[...]
         for v in range(2):
-            spb[:, chunk(v)] = down(sum_levels(pbar[:, v * LANES : (v + 1) * LANES], p_all))
+            spb[:, chunk(v)] = down(sum_levels(pbar[:, v * LANES : (v + 1) * LANES] * p_all))
         finals = []
         for r in range(windows):
             for d in range(2):
@@ -496,19 +543,16 @@
                 copy.start()
                 finals.append(copy)
 
+        bfix[...] = back_east
+        both = jnp.broadcast_to(jnp.sum(kcol[...] * pcol[...], axis=0, keepdims=True), (8, LANES))
         for v in range(NV):
-            mu[:, chunk(v)] = mu[:, chunk(v)] + unpacked(back_east, v // 16, v % 16, 61, l64 >= 61)
-        both = jnp.broadcast_to(jnp.sum(kcol[...] * pcol[...], axis=0, keepdims=True), (8, LANES))
-
-        @pl.loop(0, NV)
-        def _(v):
-            m = mu[:, chunk(v)] * p_all
+            whole = mu[:, chunk(v)] + jnp.where(l64 >= 61, roll(bfix[:, pl.ds(v // 16 * LANES, LANES)], 61 - 4 * (v % 16)), 0.0)
+            m = whole * p_all
             a1, a2, a3 = coefs(cx[:, chunk(v)])
             f = m - jnp.where(l64 >= 1, roll(m, 1), 0.0)
-            ones = jnp.ones((rows, LANES), F32)
-            s0 = sum_levels(m, ones)
-            s1, s2, s3 = sum_levels(f * a1, ones), sum_levels(f * a2, ones), sum_levels(f * a3, ones)
-            z1, z2, z3 = sum_levels(m * a1, ones), sum_levels(m * a2, ones), sum_levels(m * a3, ones)
+            s0 = sum_levels(m)
+            s1, s2, s3 = sum_levels(f * a1), sum_levels(f * a2), sum_levels(f * a3)
+            z1, z2, z3 = sum_levels(m * a1), sum_levels(m * a2), sum_levels(m * a3)
             res = s0 + jnp.where(l64_8 < 63, roll(s1, -1), -z1)
             res = res + jnp.where(l64_8 < 62, roll(s2, -2), jnp.where(l64_8 == 62, -roll(z2, -1), 0.0))
             res = res + jnp.where(l64_8 < 61, roll(s3, -3), jnp.where(l64_8 == 61, -roll(z3, -2), 0.0))
@@ -569,7 +613,7 @@
         in_specs=[anywhere] * 8 + [pl.BlockSpec(memory_space=pltpu.SMEM)],
         out_specs=pl.BlockSpec(memory_space=pltpu.VMEM),
         scratch_shapes=[
-            vm((levels * NV, LANES), F32),
+            vm((rows * NV, LANES), F32),
             vm((rows, CELLS), F32),
             vm((rows, CELLS + 256), F32),
             vm((rows, CELLS), F32),
@@ -584,10 +628,13 @@
             vm((rows, LANES), F32),
             vm((rows, LANES), F32),
             vm((8, CELLS), F32),
+            vm((8, CELLS), F32),
+            vm((rows, 256), F32),
             vm((512, 512), BF16),
             vm((512, 512), BF16),
             vm((512, 512), BF16),
             vm((512, 512), BF16),
+            vm((rows, 256), F32),
             vm((rows, 256), F32),
             vm((rows, 256), F32),
             vm((rows, 256), F32),
@@ -602,7 +649,7 @@
             vm((NV, LANES), F32),
             vm((windows - 1, per, LANES), F32),
             vm((NV, LANES), F32),
-            dma((8,)),
+            dma((7 + rows // 8,)),
             dma((4, 2)),
             dma((4, 2)),
             dma((2,)),

time: 52.8 us -> 35.9 us (0.68)
  Pallas kernels: 51.3 us -> 34.5 us
    pallas_call x1, Pallas kernels: 51.3 us -> 34.5 us  [body(): pl.pallas_call(run, out_shape=jax.ShapeDtypeStruct((1, 2 * per, SIDE), F3...]
where the time goes in v2:
time: 35.9 us; the launch traced here: 35.8 us
  Pallas kernels  34.5 us (96%)
  local copies, waits for them, and re-layouts  1.3 us (4%)
    pallas_call x1, Pallas kernels, body(): pl.pallas_call(run, out_shape=jax.ShapeDtypeStruct((1, 2 * per, SIDE), F3...  34.5 us
    unnamed x1, local copies, waits for them, and re-layouts  1.3 us

profile of v2, /device:TPU:1, one launch (start us, length us, event | category | flops | bytes accessed | tf_op | source)
XLA Modules:
  0.0 35.8 jit_solution(17615650336197542454)
XLA Ops:
  0.0 34.5 %shard_map.91 = f32[1,16,64]{2,1,0:T(8,128)} custom-call(f32[1152,128]{1,0:T(8,128)} %bitcast.3, bf16[1,1,36,4096]{3,2,1,0:T(8,128)(2,1)} %cx_h.1, bf16[1,1,36,4096]{3,2,1,0:T(8,128)(2,1)} %cy_h.1, f32[1,1,64,64]{3,2,1,0:T(8,128)} %obs_h.1, f32[1,1,64,64]{3,2,1,0:T(8,128)} %pre_h.1, f32[1,36]{1,0:T(1,128)} %bitcast.4, f32[1,36]{1,0:T(1,128)} %bitcast.5, ...), custom_call_target="tpu_custom_call" | custom-call | tf_op jit(solution)/shard_map/pallas_call | solution.py:610
  34.5 1.3 %copy.11 = f32[1,16,64]{2,1,0:T(8,128)} copy(f32[1,16,64]{2,1,0:T(8,128)} %shard_map.91) | data formatting | bytes 8192

commit v3 on v2

--- a/solution.py
+++ b/solution.py
@@ -52,9 +52,9 @@
         init_h, cx_h, cy_h, obs_h, pre_h, ker_h, pro_h, emi_h, edges,
         out,
         qi, q, bx, mu, cx, cy, cxb, cyb, sq, sq2, flat, kp, kcol, pcol, gf, df, bfix,
-        wx, wxt, wy, wyt, epack, ewrap, cpack, dbuf,
-        sbuf, rbuf, sset, rset, scol, rcol, spb, rpb, gint, rg, fin,
-        in_sem, s_sem, r_sem, sset_sem, rset_sem, scol_sem, rcol_sem, spb_sem, rpb_sem, sg_sem, rg_sem,
+        wx, wxt, wy, wyt, epack, ewrap, cyp, cpack, dbuf,
+        sbuf, rbuf, sy, ry, sdc, rdc, sset, rset, scol, rcol, spb, rpb, gint, rg, fin,
+        in_sem, s_sem, r_sem, sset_sem, rset_sem, scol_sem, rcol_sem, spb_sem, rpb_sem, sg_sem, rg_sem, near_sem,
     ):
         w = lax.axis_index("win")
         t = lax.axis_index("tile")
@@ -89,14 +89,8 @@
             load.start()
 
         barrier = pltpu.get_barrier_semaphore()
-        partners = []
-        near = {1, tiles // 4, tiles - 1, tiles - tiles // 4}
-        far = near | {2, tiles - 2, tiles // 2}
-        for off in sorted(far):
-            partners.append((w, fwd(off)))
-        for r in range(1, windows):
-            for off in sorted(near | {0}):
-                partners.append((win_of(r), fwd(off)))
+        partners = [(w, fwd(off)) for off in (1, tiles // 4, tiles - tiles // 4, tiles - 1)]
+        partners += [(win_of(r), t) for r in range(1, windows)]
         for who in partners:
             pl.semaphore_signal(barrier, inc=1, device_id=who, device_id_type=MESH)
 
@@ -173,6 +167,39 @@
                 copies.append(send(stage, d, fwd(offs[d])))
             pending.extend(copies)
             return copies
+
+        pairs, odd = tiles_of // 2, tiles_of % 2
+        fold = odd == 1 and 0 < levels % 8 <= 4
+        packed = 8 * (tiles_of + pairs + (odd == 1 and not fold))
+        sub8 = lax.broadcasted_iota(I32, (8, LANES), 0)
+
+        def squeeze(x):
+            far, near_two = x[:, :LANES], x[:, LANES:]
+            pieces = [near_two[8 * i : 8 * i + 8] for i in range(tiles_of)]
+            extra = [
+                jnp.where(low8, roll(far[16 * i : 16 * i + 8], SIDE), far[16 * i + 8 : 16 * i + 16]) for i in range(pairs)
+            ]
+            if odd:
+                tail = roll(far[rows - 8 :], SIDE)
+                if fold:
+                    pieces[-1] = jnp.where(sub8 < 4, pieces[-1], pltpu.roll(tail, 4, 0))
+                else:
+                    extra.append(tail)
+            return jnp.concatenate(pieces + extra, axis=0)
+
+        def unsqueeze(x):
+            near_two = [x[8 * i : 8 * i + 8] for i in range(tiles_of)]
+            far = []
+            for i in range(pairs):
+                both_ = x[rows + 8 * i : rows + 8 * i + 8]
+                far += [both_, roll(both_, SIDE)]
+            if odd:
+                if fold:
+                    far.append(jnp.where(sub8 < 4, pltpu.roll(near_two[-1], 4, 0), 0.0))
+                    near_two[-1] = jnp.where(sub8 < 4, near_two[-1], 0.0)
+                else:
+                    far.append(x[rows + 8 * pairs : rows + 8 * pairs + 8])
+            return jnp.concatenate(near_two, axis=0), jnp.concatenate(far, axis=0)
 
         def received(copies, stage):
             for copy in copies:
@@ -221,17 +248,21 @@
             sbuf[0, d] = strips[:, d * 256 : (d + 1) * 256]
         pl.semaphore_wait(barrier, len(partners))
         first = [send(0, d, fwd(off_x[d])) for d in range(2)]
+        for who in partners:
+            pl.semaphore_signal(near_sem, inc=1, device_id=who, device_id_type=MESH)
         pending.extend(first)
-
-        loads[0].wait()
-        loads[1].wait()
-        for c, cb in ((cx, cxb), (cy, cyb)):
+        build(wy, 3, off_y, 1, False)
+
+        def widen(c, cb):
             c[pl.ds(levels, rows - levels), :] = jnp.zeros((rows - levels, CELLS), F32)
 
             @pl.loop(0, NV // 8)
-            def _(v, c=c, cb=cb):
+            def _(v):
                 some = pl.ds(pl.multiple_of(v * 8 * LANES, 8 * LANES), 8 * LANES)
                 c[pl.ds(0, levels), some] = cb[:, some].astype(F32)
+
+        loads[0].wait()
+        widen(cx, cxb)
 
         def x_interior():
             @pl.loop(0, tiles_of)
@@ -253,6 +284,98 @@
 
         x_interior()
 
+        pack(cpack, cx, 0, 0)
+        part = lanes_of((rows, 256)) & 3
+        p1, p2, p3 = coefs(cpack[...])
+        west1 = jnp.where(part == 0, p1, 0.0)
+        west2 = jnp.where(part <= 1, p2, 0.0)
+        west3 = jnp.where(part <= 2, p3, 0.0)
+        cpack3 = (west1, west2, west3)
+
+        def west_change(panel):
+            panel = panel - ewrap[...]
+            f = panel * cpack3[2] + roll2(panel, -1) * cpack3[1] + roll2(panel, -2) * cpack3[0]
+            return jnp.where(part < 3, f - roll2(f, -1), 0.0)
+
+        def y_flux(qv_r, q1, q1_r, q2_r, c):
+            a1, a2, a3 = coefs(c)
+            s1 = jnp.where(low, q1_r, qv_r)
+            return s1 * a1 + q1 * a2 + jnp.where(low, q2_r, q1_r) * a3
+
+        def y_interior(here_rows, finish, changed):
+            none = jnp.zeros((8, LANES), F32)
+            xs, rs, turned, outlet = {-1: none, -2: none}, {-1: none, -2: none}, {}, None
+            done = {}
+            lowest = 2 if changed else 0
+            for v in range(NV):
+                xs[v] = bx[here_rows, chunk(v + 2)]
+                if changed:
+                    change = dbuf[here_rows, pl.ds(v // 16 * LANES, LANES)]
+                    xs[v] = xs[v] + jnp.where(l64_8 < 3, roll(change, -4 * (v % 16)), 0.0)
+                    if v < 3:
+                        bx[here_rows, chunk(v + 2)] = xs[v]
+                rs[v] = roll(xs[v], SIDE)
+                if v < lowest:
+                    continue
+                a1, a2, a3 = coefs(cy[here_rows, chunk(v)])
+                flux = jnp.where(low8, rs[v - 1], rs[v]) * a1 + xs[v - 1] * a2 + jnp.where(low8, rs[v - 2], rs[v - 1]) * a3
+                turned[v] = roll(flux, SIDE)
+                done[v] = xs[v] + flux
+                if v > lowest:
+                    finish(v - 1, done[v - 1] - jnp.where(low8, turned[v - 1], turned[v]))
+                if v == NV - 1:
+                    outlet = xs[v] * a1 + jnp.where(low8, rs[v - 1], rs[v]) * a2 + xs[v - 1] * a3
+                    finish(v, done[v] - jnp.where(low8, turned[v], outlet))
+
+        def y_first(ta, pb):
+            q0_, q1_, q2_ = bx[:, chunk(2)], bx[:, chunk(3)], bx[:, chunk(4)]
+            t0, t1, t2 = roll(q0_, SIDE), roll(q1_, SIDE), roll(q2_, SIDE)
+            tb = roll(pb, SIDE)
+            above = roll(y_flux(t2, q1_, t1, t0, cy[:, chunk(2)]), SIDE)
+            f1 = y_flux(t1, q0_, t0, tb, cy[:, chunk(1)])
+            f0 = y_flux(t0, pb, tb, ta, cy[:, chunk(0)])
+            g1, g0 = roll(f1, SIDE), roll(f0, SIDE)
+            n1 = q1_ + f1 - jnp.where(low, g1, above) + emitted(1)
+            n0 = q0_ + f0 - jnp.where(low, g0, g1) + emitted(0)
+            return n0, n1
+
+        def emitted(v):
+            return pcol[...] * jnp.concatenate([flat[0, :, chunk(v)]] * (rows // 8), axis=0)
+
+        def sum_levels(x):
+            acc = x[0:8]
+            for i in range(1, rows // 8):
+                acc = acc + x[8 * i : 8 * i + 8]
+            return acc
+
+        def down(x):
+            return jnp.broadcast_to(jnp.sum(x, axis=0, keepdims=True), (8, LANES))
+
+        def tall(x):
+            return jnp.concatenate([x] * (rows // 8), axis=0)
+
+        panel = received(first, 0)
+        dbuf[...] = west_change(panel)
+        change = dbuf[:, pl.ds(LANES, LANES)]
+        ends_now = [
+            bx[:, chunk(v + 2)] + jnp.where(l64 < 3, roll(change, -4 * (v % 16)), 0.0) for v in (NV - 2, NV - 1)
+        ]
+        res = permute(jnp.concatenate([epack[...]] + ends_now, axis=1), wy)
+        for d in range(2):
+            sy[d] = squeeze(res[:, d * 256 : (d + 1) * 256])
+        pl.semaphore_wait(near_sem, len(partners))
+        y1 = []
+        for d in range(2):
+            copy = pltpu.make_async_remote_copy(
+                src_ref=sy.at[d], dst_ref=ry.at[d], send_sem=s_sem.at[1, d], recv_sem=r_sem.at[1, d],
+                device_id=(w, fwd(off_y[d])), device_id_type=MESH,
+            )
+            copy.start()
+            y1.append(copy)
+        pending.extend(y1)
+
+        loads[1].wait()
+        widen(cy, cyb)
         for i in range(3):
             loads[4 + i].wait()
             x = sq[i]
@@ -280,9 +403,14 @@
         inv = 1.0 / jnp.sum(kp[0], axis=1, keepdims=True)
         inv8 = jnp.broadcast_to(inv, (8, LANES))
 
-        sset[pl.ds(0, rows), :] = cy[:, pl.ds(0, 256)]
+
+        sset[pl.ds(0, packed), :] = squeeze(
+            jnp.concatenate([roll(cy[:, chunk(1)], SIDE), cy[:, chunk(0)]], axis=1)
+        )
+        sset[pl.ds(packed + 4, 4), :] = jnp.zeros((4, LANES), F32)
         for i in range(2):
-            sset[pl.ds(rows + 8 * i, 8), :] = flat[1 + i, :, pl.ds(0, 256)]
+            for v in range(2):
+                sset[pl.ds(packed + 2 * i + v, 1), :] = flat[1 + i, pl.ds(0, 1), chunk(v)]
         sets = []
         for d in range(2):
             copy = pltpu.make_async_remote_copy(
@@ -292,84 +420,6 @@
             copy.start()
             sets.append(copy)
 
-        build(wy, 3, off_y, 1, False)
-
-        pack(cpack, cx, 0, 0)
-        part = lanes_of((rows, 256)) & 3
-        p1, p2, p3 = coefs(cpack[...])
-        west1 = jnp.where(part == 0, p1, 0.0)
-        west2 = jnp.where(part <= 1, p2, 0.0)
-        west3 = jnp.where(part <= 2, p3, 0.0)
-        cpack3 = (west1, west2, west3)
-
-        def west_change(panel):
-            panel = panel - ewrap[...]
-            f = panel * cpack3[2] + roll2(panel, -1) * cpack3[1] + roll2(panel, -2) * cpack3[0]
-            return jnp.where(part < 3, f - roll2(f, -1), 0.0)
-
-        def y_flux(qv_r, q1, q1_r, q2_r, c):
-            a1, a2, a3 = coefs(c)
-            s1 = jnp.where(low, q1_r, qv_r)
-            return s1 * a1 + q1 * a2 + jnp.where(low, q2_r, q1_r) * a3
-
-        def y_interior(here_rows, finish, fixed=0):
-            changes = [dbuf[here_rows, pl.ds(g * LANES, LANES)] for g in range(2)]
-            xs, rs, turned, outlet = {}, {}, {}, None
-            done = {}
-            for v in range(NV):
-                xs[v] = bx[here_rows, chunk(v + 2)]
-                if v >= fixed:
-                    xs[v] = xs[v] + jnp.where(l64_8 < 3, roll(changes[v // 16], -4 * (v % 16)), 0.0)
-                if fixed <= v < 3:
-                    bx[here_rows, chunk(v + 2)] = xs[v]
-                rs[v] = roll(xs[v], SIDE)
-                if v < 2:
-                    continue
-                a1, a2, a3 = coefs(cy[here_rows, chunk(v)])
-                flux = jnp.where(low8, rs[v - 1], rs[v]) * a1 + xs[v - 1] * a2 + jnp.where(low8, rs[v - 2], rs[v - 1]) * a3
-                turned[v] = roll(flux, SIDE)
-                done[v] = xs[v] + flux
-                if v > 2:
-                    finish(v - 1, done[v - 1] - jnp.where(low8, turned[v - 1], turned[v]))
-                if v == NV - 1:
-                    outlet = xs[v] * a1 + jnp.where(low8, rs[v - 1], rs[v]) * a2 + xs[v - 1] * a3
-                    finish(v, done[v] - jnp.where(low8, turned[v], outlet))
-
-        def y_first(pa, pb):
-            q0_, q1_, q2_ = bx[:, chunk(2)], bx[:, chunk(3)], bx[:, chunk(4)]
-            t0, t1, t2 = roll(q0_, SIDE), roll(q1_, SIDE), roll(q2_, SIDE)
-            ta, tb = roll(pa, SIDE), roll(pb, SIDE)
-            above = roll(y_flux(t2, q1_, t1, t0, cy[:, chunk(2)]), SIDE)
-            f1 = y_flux(t1, q0_, t0, tb, cy[:, chunk(1)])
-            f0 = y_flux(t0, pb, tb, ta, cy[:, chunk(0)])
-            g1, g0 = roll(f1, SIDE), roll(f0, SIDE)
-            n1 = q1_ + f1 - jnp.where(low, g1, above) + emitted(1)
-            n0 = q0_ + f0 - jnp.where(low, g0, g1) + emitted(0)
-            return n0, n1
-
-        def emitted(v):
-            return pcol[...] * jnp.concatenate([flat[0, :, chunk(v)]] * (rows // 8), axis=0)
-
-        def sum_levels(x):
-            acc = x[0:8]
-            for i in range(1, rows // 8):
-                acc = acc + x[8 * i : 8 * i + 8]
-            return acc
-
-        def down(x):
-            return jnp.broadcast_to(jnp.sum(x, axis=0, keepdims=True), (8, LANES))
-
-        def tall(x):
-            return jnp.concatenate([x] * (rows // 8), axis=0)
-
-        panel = received(first, 0)
-        dbuf[...] = west_change(panel)
-        change = dbuf[:, pl.ds(LANES, LANES)]
-        ends_now = [
-            bx[:, chunk(v + 2)] + jnp.where(l64 < 3, roll(change, -4 * (v % 16)), 0.0) for v in (NV - 2, NV - 1)
-        ]
-        y1 = send_strips(1, epack[...], jnp.concatenate(ends_now, axis=1), wy, off_y)
-
         @pl.loop(0, tiles_of)
         def _(i):
             here_rows = tile_rows(i)
@@ -381,20 +431,70 @@
                 q[here_rows, chunk(v)] = res
                 acc[v // 16] = put(acc[v // 16], res, v, 61)
 
-            y_interior(here_rows, finish)
+            y_interior(here_rows, finish, True)
             epack[here_rows, pl.ds(0, LANES)] = acc[0]
             epack[here_rows, pl.ds(LANES, LANES)] = acc[1]
 
-        panel = received(y1, 1)
-        for v, res in enumerate(y_first(panel[:, :LANES], panel[:, LANES:])):
+        build(wyt, 3, off_y, 1, True)
+        build(wxt, 0, off_x, 0, True)
+        pack(cyp, cy, 0, 0)
+        for copy in y1:
+            copy.wait_recv()
+        near_two, far_one = unsqueeze(ry[0] + ry[1])
+        east = epack[:, pl.ds(0, LANES)]
+        for v, res in enumerate(y_first(far_one, near_two)):
             q[:, chunk(v)] = res
-        epack[:, pl.ds(0, LANES)] = pack_group(q, 0, 61, 0, range(2), epack[:, pl.ds(0, LANES)])
+            east = jnp.where(((l64 >> 2) == v) & ((l64 & 3) < 3), roll(res, 4 * v - 61), east)
+        epack[:, pl.ds(0, LANES)] = east
 
         x2 = send_strips(2, epack[...], q[:, pl.ds(CELLS - 256, 256)], wx, off_x)
         x_interior()
-        build(wyt, 3, off_y, 1, True)
         for copy in sets:
             copy.wait_recv()
+
+        gf[...] = jnp.zeros((8, CELLS), F32)
+
+        @pl.loop(0, tiles_of)
+        def _(i):
+            here_rows = tile_rows(i)
+            share, weight = pcol[here_rows, :], kcol[here_rows, :]
+
+            def finish(v, res):
+                gf[:, chunk(v)] = gf[:, chunk(v)] + (res + share * flat[0, :, chunk(v)]) * weight
+
+            y_interior(here_rows, finish, False)
+
+        def slots(x):
+            index = lanes_of(x.shape)
+            return (index >> 6) & 1, (index >> 2) & 15
+
+        def shift_down(x):
+            high, u = slots(x[0])
+            res = []
+            for g in range(2):
+                over = roll(x[g - 1], 4) if g > 0 else jnp.zeros_like(x[0])
+                res.append(jnp.where(high == 1, roll(x[g], SIDE), jnp.where(u == 0, over, roll(x[g], 68))))
+            return res
+
+        def shift_down2(x):
+            u = slots(x[0])[1]
+            res = []
+            for g in range(2):
+                over = roll(x[g - 1], 68) if g > 0 else jnp.zeros_like(x[0])
+                res.append(jnp.where(u == 0, over, roll(x[g], 4)))
+            return res
+
+        def shift_up(x, after):
+            high, u = slots(x[0])
+            res = []
+            for g in range(2):
+                over = roll(x[g + 1], 124) if g == 0 else after
+                res.append(jnp.where(high == 0, roll(x[g], SIDE), jnp.where(u == 15, over, roll(x[g], 60))))
+            return res
+
+        ca = [coefs(cyp[:, pl.ds(g * LANES, LANES)]) for g in range(2)]
+        k_all = kcol[...]
+        zero = jnp.zeros((rows, LANES), F32)
 
         panel = received(x2, 2)
         dbuf[...] = west_change(panel)
@@ -402,18 +502,23 @@
         ends_now = [
             bx[:, chunk(v + 2)] + jnp.where(l64 < 3, roll(change, -4 * (v % 16)), 0.0) for v in (NV - 2, NV - 1)
         ]
-        y2 = send_strips(3, epack[...], jnp.concatenate(ends_now, axis=1), wy, off_y)
+        panels = permute(jnp.concatenate([epack[...]] + ends_now, axis=1), wy)
 
         def misfit_weight(col, v_obs, v_pre):
             return v_pre * (col * inv8 - v_obs) * inv8
 
-        k_all = kcol[...]
-        zero = jnp.zeros((rows, LANES), F32)
-        change = dbuf[:, pl.ds(0, LANES)]
-        for v in range(3):
-            bx[:, chunk(v + 2)] = bx[:, chunk(v + 2)] + jnp.where(l64 < 3, roll(change, -4 * v), 0.0)
-        for v, n in enumerate(y_first(zero, zero)):
-            scol[:, chunk(v)] = down(sum_levels(n * k_all))
+        new = [dbuf[:, pl.ds(g * LANES, LANES)] for g in range(2)]
+        s1, s2 = shift_down(new), shift_down2(new)
+        s3 = shift_down(s2)
+        flow = [s1[g] * ca[g][0] + s2[g] * ca[g][1] + s3[g] * ca[g][2] for g in range(2)]
+        out_flow = shift_up(flow, new[1] * ca[1][0] + s1[1] * ca[1][1] + s2[1] * ca[1][2])
+        gained = [sum_levels((new[g] + flow[g] - out_flow[g]) * k_all) for g in range(2)]
+
+        def column(v):
+            return down(gf[:, chunk(v)] + jnp.where(l64_8 < 3, roll(gained[v // 16], -4 * (v % 16)), 0.0))
+
+        for v in range(2):
+            scol[:, chunk(v)] = column(v)[0:1]
         cols = []
         for d in range(2):
             copy = pltpu.make_async_remote_copy(
@@ -423,17 +528,29 @@
             copy.start()
             cols.append(copy)
 
-        gf[...] = jnp.zeros((8, CELLS), F32)
-
-        @pl.loop(0, tiles_of)
-        def _(i):
-            here_rows = tile_rows(i)
-            share, weight = pcol[here_rows, :], kcol[here_rows, :]
-
-            def finish(v, res):
-                gf[:, chunk(v)] = gf[:, chunk(v)] + (res + share * flat[0, :, chunk(v)]) * weight
-
-            y_interior(here_rows, finish, 3)
+        effects, edge = [], []
+        for d in range(2):
+            pa, pb = panels[:, d * 256 : d * 256 + LANES], panels[:, d * 256 + LANES : d * 256 + 256]
+            ra, rb = roll(pa, SIDE), roll(pb, SIDE)
+            c0, c1 = unsqueeze(rset[d, pl.ds(0, packed), :])
+            z1, z2, z3 = coefs(c0)
+            o3 = coefs(c1)[2]
+            edge.append((z1, z2, z3, o3))
+            h0 = jnp.where(low, rb, 0.0) * z1 + pb * z2 + jnp.where(low, ra, rb) * z3
+            h1 = jnp.where(low, rb, 0.0) * o3
+            k0, k1 = roll(h0, SIDE), roll(h1, SIDE)
+            d0 = h0 - jnp.where(low, k0, k1)
+            d1 = h1 - jnp.where(low, k1, 0.0)
+            effects.append((down(sum_levels(d0 * k_all)), down(sum_levels(d1 * k_all))))
+            for v in range(2):
+                sdc[d, :, chunk(v)] = effects[d][v][0:1]
+        for d in range(2):
+            copy = pltpu.make_async_remote_copy(
+                src_ref=sdc.at[d], dst_ref=rdc.at[d], send_sem=s_sem.at[3, d], recv_sem=r_sem.at[3, d],
+                device_id=(w, fwd(off_y[d])), device_id_type=MESH,
+            )
+            copy.start()
+            pending.append(copy)
 
         def weigh(v, col):
             gf[:, chunk(v)] = misfit_weight(col, flat[1, :, chunk(v)], flat[2, :, chunk(v)])
@@ -444,7 +561,8 @@
             return here - jnp.where(low8, before, roll(here, SIDE))
 
         for v in range(2, NV):
-            weigh(v, down(gf[:, chunk(v)]))
+            weigh(v, column(v))
+        gf[:, pl.ds(0, 256)] = jnp.zeros((8, 256), F32)
         for v in range(2, NV):
             df[:, chunk(v)] = slope(v)
 
@@ -476,28 +594,17 @@
             dbuf[here_rows, pl.ds(0, LANES)] = acc[0]
             dbuf[here_rows, pl.ds(LANES, LANES)] = acc[1]
 
-        build(wxt, 0, off_x, 0, True)
-
         bars = []
         for d in range(2):
             cols[d].wait_recv()
-            pa, pb = sbuf[3, d, :, pl.ds(0, LANES)], sbuf[3, d, :, pl.ds(LANES, LANES)]
-            ra, rb = roll(pa, SIDE), roll(pb, SIDE)
-            c0, c1 = rset[d, pl.ds(0, rows), pl.ds(0, LANES)], rset[d, pl.ds(0, rows), pl.ds(LANES, LANES)]
-            z1, z2, z3 = coefs(c0)
-            o1, o2, o3 = coefs(c1)
-            h0 = jnp.where(low, rb, 0.0) * z1 + pb * z2 + jnp.where(low, ra, rb) * z3
-            h1 = jnp.where(low, rb, 0.0) * o3
-            k0, k1 = roll(h0, SIDE), roll(h1, SIDE)
-            d0 = h0 - jnp.where(low, k0, k1)
-            d1 = h1 - jnp.where(low, k1, 0.0)
-            w0 = misfit_weight(
-                rcol[d, :, chunk(0)] + down(sum_levels(d0 * k_all)),
-                rset[d, pl.ds(rows, 8), chunk(0)], rset[d, pl.ds(rows + 8, 8), chunk(0)],
-            )
-            w1 = misfit_weight(
-                rcol[d, :, chunk(1)] + down(sum_levels(d1 * k_all)),
-                rset[d, pl.ds(rows, 8), chunk(1)], rset[d, pl.ds(rows + 8, 8), chunk(1)],
+            z1, z2, z3, o3 = edge[d]
+            w0, w1 = (
+                misfit_weight(
+                    jnp.broadcast_to(rcol[d, :, chunk(v)], (8, LANES)) + effects[d][v],
+                    jnp.broadcast_to(rset[d, pl.ds(packed + v, 1), :], (8, LANES)),
+                    jnp.broadcast_to(rset[d, pl.ds(packed + 2 + v, 1), :], (8, LANES)),
+                )
+                for v in range(2)
             )
             turned = roll(w0, SIDE)
             bar0 = k_all * tall(w0 - jnp.where(low8, 0.0, turned))
@@ -509,9 +616,10 @@
         back = permute(jnp.concatenate(bars, axis=1), wyt)
         back_east, back_north = back[:, :256], back[:, 256:]
 
-        panel = received(y2, 3)
-        for v, n in enumerate(y_first(panel[:, :LANES], panel[:, LANES:])):
-            weigh(v, down(sum_levels(n * k_all)))
+        for copy in pending[-2:]:
+            copy.wait_recv()
+        for v in range(2):
+            weigh(v, jnp.broadcast_to(scol[:, chunk(v)] + rdc[0, :, chunk(v)] + rdc[1, :, chunk(v)], (8, LANES)))
         made = {}
         for v in range(4):
             bar = k_all * tall(slope(v))
@@ -532,7 +640,7 @@
         pbar = diff * cpack3[2] + roll2(diff * cpack3[1], 1) + roll2(diff * cpack3[0], 2)
         p_all = pcol[...]
         for v in range(2):
-            spb[:, chunk(v)] = down(sum_levels(pbar[:, v * LANES : (v + 1) * LANES] * p_all))
+            spb[:, chunk(v)] = down(sum_levels(pbar[:, v * LANES : (v + 1) * LANES] * p_all))[0:1]
         finals = []
         for r in range(windows):
             for d in range(2):
@@ -545,29 +653,32 @@
 
         bfix[...] = back_east
         both = jnp.broadcast_to(jnp.sum(kcol[...] * pcol[...], axis=0, keepdims=True), (8, LANES))
-        for v in range(NV):
-            whole = mu[:, chunk(v)] + jnp.where(l64 >= 61, roll(bfix[:, pl.ds(v // 16 * LANES, LANES)], 61 - 4 * (v % 16)), 0.0)
-            m = whole * p_all
-            a1, a2, a3 = coefs(cx[:, chunk(v)])
-            f = m - jnp.where(l64 >= 1, roll(m, 1), 0.0)
-            s0 = sum_levels(m)
-            s1, s2, s3 = sum_levels(f * a1), sum_levels(f * a2), sum_levels(f * a3)
-            z1, z2, z3 = sum_levels(m * a1), sum_levels(m * a2), sum_levels(m * a3)
-            res = s0 + jnp.where(l64_8 < 63, roll(s1, -1), -z1)
-            res = res + jnp.where(l64_8 < 62, roll(s2, -2), jnp.where(l64_8 == 62, -roll(z2, -1), 0.0))
-            res = res + jnp.where(l64_8 < 61, roll(s3, -3), jnp.where(l64_8 == 61, -roll(z3, -2), 0.0))
-            gint[pl.ds(v, 1), :] = (down(res) + both * gf[:, chunk(v)])[0:1]
-
         sums = []
-        for r in range(1, windows):
+        for r in [*range(1, windows), 0]:
             to = win_of(r)
-            copy = pltpu.make_async_remote_copy(
-                src_ref=gint.at[pl.ds(pl.multiple_of(to * per, per), per), :], dst_ref=rg.at[r - 1],
-                send_sem=sg_sem.at[r - 1], recv_sem=rg_sem.at[r - 1],
-                device_id=(to, t), device_id_type=MESH,
-            )
-            copy.start()
-            sums.append(copy)
+            side = lax.div(to * per, 16)
+            east = bfix[:, chunk(side)]
+            if per < 16:
+                east = jnp.where(lax.rem(to * per, 16) == 8, roll(east, -32), east)
+            for k in range(per):
+                v = to * per + k
+                whole = mu[:, chunk(v)] + jnp.where(l64 >= 61, roll(east, 61 - 4 * k), 0.0)
+                m = whole * p_all
+                c = cx[:, chunk(v)]
+                a1, a2, a3 = coefs(jnp.where(l64 == 0, roll(c, 1), c))
+                f = jnp.where(l64 == 0, 0.0, m) - roll(m, 1)
+                s0 = sum_levels(m)
+                s1, s2, s3 = sum_levels(f * a1), sum_levels(f * a2), sum_levels(f * a3)
+                res = s0 + roll(s1, -1) + jnp.where(l64_8 < 63, roll(s2, -2), 0.0) + jnp.where(l64_8 < 62, roll(s3, -3), 0.0)
+                gint[r, pl.ds(k, 1), :] = (down(res) + both * gf[:, chunk(v)])[0:1]
+            if r > 0:
+                copy = pltpu.make_async_remote_copy(
+                    src_ref=gint.at[r], dst_ref=rg.at[r - 1],
+                    send_sem=sg_sem.at[r - 1], recv_sem=rg_sem.at[r - 1],
+                    device_id=(to, t), device_id_type=MESH,
+                )
+                copy.start()
+                sums.append(copy)
 
         for copy in finals:
             copy.wait_recv()
@@ -576,7 +687,7 @@
             acc = rpb[d, 0]
             for r in range(1, windows):
                 acc = acc + rpb[d, r]
-            halves.append(acc)
+            halves.append(jnp.broadcast_to(acc, (8, 256)))
         ends = permute(jnp.concatenate(halves, axis=1), wxt)
         for v in range(NV):
             g, u = v // 16, v % 16
@@ -586,7 +697,7 @@
                 row = row + ends[:, at : at + LANES]
             fin[pl.ds(v, 1), :] = row[0:1]
         mine = pl.ds(pl.multiple_of(w * per, per), per)
-        total = gint[mine, :] + fin[mine, :]
+        total = gint[0] + fin[mine, :]
         for copy in sums:
             copy.wait_recv()
         for r in range(1, windows):
@@ -604,12 +715,14 @@
     levels = initial.shape[2]
     windows = lax.axis_size("win")
     run, rows, per = make_kernel(levels, windows)
+    tiles_of = rows // 8
+    packed = 8 * (tiles_of + tiles_of // 2 + (tiles_of % 2 == 1 and not 0 < levels % 8 <= 4))
     vm = pltpu.VMEM
     dma = pltpu.SemaphoreType.DMA
     anywhere = pl.BlockSpec(memory_space=pl.ANY)
     return pl.pallas_call(
         run,
-        out_shape=jax.ShapeDtypeStruct((1, 2 * per, SIDE), F32),
+        out_shape=pltpu.VMEM((1, 2 * per, SIDE), F32),
         in_specs=[anywhere] * 8 + [pl.BlockSpec(memory_space=pltpu.SMEM)],
         out_specs=pl.BlockSpec(memory_space=pltpu.VMEM),
         scratch_shapes=[
@@ -638,15 +751,20 @@
             vm((rows, 256), F32),
             vm((rows, 256), F32),
             vm((rows, 256), F32),
+            vm((rows, 256), F32),
             vm((4, 2, rows, 256), F32),
             vm((4, 2, rows, 256), F32),
-            vm((rows + 16, 256), F32),
-            vm((2, rows + 16, 256), F32),
-            vm((8, 256), F32),
-            vm((2, 8, 256), F32),
-            vm((8, 256), F32),
-            vm((2, windows, 8, 256), F32),
-            vm((NV, LANES), F32),
+            vm((2, packed, LANES), F32),
+            vm((2, packed, LANES), F32),
+            vm((2, 1, 256), F32),
+            vm((2, 1, 256), F32),
+            vm((packed + 8, LANES), F32),
+            vm((2, packed + 8, LANES), F32),
+            vm((1, 256), F32),
+            vm((2, 1, 256), F32),
+            vm((1, 256), F32),
+            vm((2, windows, 1, 256), F32),
+            vm((windows, per, LANES), F32),
             vm((windows - 1, per, LANES), F32),
             vm((NV, LANES), F32),
             dma((7 + rows // 8,)),
@@ -660,6 +778,7 @@
             dma((2, windows)),
             dma((windows - 1,)),
             dma((windows - 1,)),
+            pltpu.SemaphoreType.REGULAR,
         ],
         compiler_params=pltpu.CompilerParams(collective_id=0, has_side_effects=True),
     )(

time: 35.9 us -> 35.8 us (level)
  local copies, waits for them, and re-layouts: 1.3 us -> 0.6 us
  Pallas kernels: 34.5 us -> 35.1 us
    unnamed x1, local copies, waits for them, and re-layouts: 1.3 us -> 0.6 us
    pallas_call x1, Pallas kernels: 34.5 us -> 35.1 us  [body(): pl.pallas_call(run, out_shape=pltpu.VMEM((1, 2 * per, SIDE), F32), in_spe...]
where the time goes in v3:
time: 35.8 us; the launch traced here: 35.7 us
  Pallas kernels  35.1 us (98%)
  local copies, waits for them, and re-layouts  0.6 us (2%)
    pallas_call x1, Pallas kernels, body(): pl.pallas_call(run, out_shape=pltpu.VMEM((1, 2 * per, SIDE), F32), in_spe...  35.1 us

profile of v3, /device:TPU:1, one launch (start us, length us, event | category | flops | bytes accessed | tf_op | source)
XLA Modules:
  0.0 35.7 jit_solution(16239335134294851253)
XLA Ops:
  0.0 35.1 %shard_map.91 = f32[1,16,64]{2,1,0:T(8,128)S(1)} custom-call(f32[1152,128]{1,0:T(8,128)} %bitcast.3, bf16[1,1,36,4096]{3,2,1,0:T(8,128)(2,1)} %cx_h.1, bf16[1,1,36,4096]{3,2,1,0:T(8,128)(2,1)} %cy_h.1, f32[1,1,64,64]{3,2,1,0:T(8,128)} %obs_h.1, f32[1,1,64,64]{3,2,1,0:T(8,128)} %pre_h.1, f32[1,36]{1,0:T(1,128)} %bitcast.4, f32[1,36]{1,0:T(1,128)} %bitcast.5, ...), custom_call_target="tpu_custom_call" | custom-call | tf_op jit(solution)/shard_map/pallas_call | solution.py:723
  35.1 0.6 %copy.11 = f32[1,16,64]{2,1,0:T(8,128)} copy(f32[1,16,64]{2,1,0:T(8,128)S(1)} %shard_map.91) | data formatting | bytes 8192

commit v4 on v3

--- a/solution.py
+++ b/solution.py
@@ -54,7 +54,7 @@
         qi, q, bx, mu, cx, cy, cxb, cyb, sq, sq2, flat, kp, kcol, pcol, gf, df, bfix,
         wx, wxt, wy, wyt, epack, ewrap, cyp, cpack, dbuf,
         sbuf, rbuf, sy, ry, sdc, rdc, sset, rset, scol, rcol, spb, rpb, gint, rg, fin,
-        in_sem, s_sem, r_sem, sset_sem, rset_sem, scol_sem, rcol_sem, spb_sem, rpb_sem, sg_sem, rg_sem, near_sem,
+        in_sem, s_sem, r_sem, sset_sem, rset_sem, scol_sem, rcol_sem, spb_sem, rpb_sem, sg_sem, rg_sem,
     ):
         w = lax.axis_index("win")
         t = lax.axis_index("tile")
@@ -89,8 +89,13 @@
             load.start()
 
         barrier = pltpu.get_barrier_semaphore()
-        partners = [(w, fwd(off)) for off in (1, tiles // 4, tiles - tiles // 4, tiles - 1)]
-        partners += [(win_of(r), t) for r in range(1, windows)]
+        partners = []
+        beside = {1, tiles // 4, tiles - 1, tiles - tiles // 4}
+        for off in sorted(beside | {2, tiles - 2, tiles // 2}):
+            partners.append((w, fwd(off)))
+        for r in range(1, windows):
+            for off in sorted(beside | {0}):
+                partners.append((win_of(r), fwd(off)))
         for who in partners:
             pl.semaphore_signal(barrier, inc=1, device_id=who, device_id_type=MESH)
 
@@ -248,8 +253,6 @@
             sbuf[0, d] = strips[:, d * 256 : (d + 1) * 256]
         pl.semaphore_wait(barrier, len(partners))
         first = [send(0, d, fwd(off_x[d])) for d in range(2)]
-        for who in partners:
-            pl.semaphore_signal(near_sem, inc=1, device_id=who, device_id_type=MESH)
         pending.extend(first)
         build(wy, 3, off_y, 1, False)
 
@@ -281,6 +284,52 @@
                     acc[v // 16] = put(acc[v // 16], res, v, 61)
                 epack[here_rows, pl.ds(0, LANES)] = acc[0]
                 epack[here_rows, pl.ds(LANES, LANES)] = acc[1]
+
+        loads[1].wait()
+        widen(cy, cyb)
+        for i in range(3):
+            loads[4 + i].wait()
+            x = sq[i]
+            sq2[i, :, pl.ds(0, SIDE)] = x
+
+        for i in range(3):
+            x = sq2[i]
+            sq2[i] = jnp.where(lanes_of((SIDE, LANES)) < SIDE, x, pltpu.roll(x, SIDE, 1))
+
+        for i in range(3):
+            @pl.loop(0, NV // 8)
+            def _(k, i=i):
+                for j in range(8):
+                    v = k * 8 + j
+                    row = jnp.where(low1, sq2[i, pl.ds(2 * v, 1), :], sq2[i, pl.ds(2 * v + 1, 1), :])
+                    flat[i, :, chunk(v)] = jnp.broadcast_to(row, (8, LANES))
+
+        loads[2].wait()
+        loads[3].wait()
+        diag = lax.broadcasted_iota(I32, (levels, levels), 0) == lax.broadcasted_iota(I32, (levels, levels), 1)
+        for i, col in ((0, kcol), (1, pcol)):
+            column = jnp.sum(jnp.where(diag, jnp.broadcast_to(kp[i], (levels, levels)), 0.0), axis=1, keepdims=True)
+            col[...] = jnp.zeros((rows, LANES), F32)
+            col[pl.ds(0, levels), :] = jnp.broadcast_to(column, (levels, LANES))
+        inv = 1.0 / jnp.sum(kp[0], axis=1, keepdims=True)
+        inv8 = jnp.broadcast_to(inv, (8, LANES))
+
+
+        sset[pl.ds(0, packed), :] = squeeze(
+            jnp.concatenate([roll(cy[:, chunk(1)], SIDE), cy[:, chunk(0)]], axis=1)
+        )
+        sset[pl.ds(packed + 4, 4), :] = jnp.zeros((4, LANES), F32)
+        for i in range(2):
+            for v in range(2):
+                sset[pl.ds(packed + 2 * i + v, 1), :] = flat[1 + i, pl.ds(0, 1), chunk(v)]
+        sets = []
+        for d in range(2):
+            copy = pltpu.make_async_remote_copy(
+                src_ref=sset, dst_ref=rset.at[d], send_sem=sset_sem.at[d], recv_sem=rset_sem.at[d],
+                device_id=(w, bwd(off_y[d])), device_id_type=MESH,
+            )
+            copy.start()
+            sets.append(copy)
 
         x_interior()
 
@@ -363,7 +412,6 @@
         res = permute(jnp.concatenate([epack[...]] + ends_now, axis=1), wy)
         for d in range(2):
             sy[d] = squeeze(res[:, d * 256 : (d + 1) * 256])
-        pl.semaphore_wait(near_sem, len(partners))
         y1 = []
         for d in range(2):
             copy = pltpu.make_async_remote_copy(
@@ -373,52 +421,6 @@
             copy.start()
             y1.append(copy)
         pending.extend(y1)
-
-        loads[1].wait()
-        widen(cy, cyb)
-        for i in range(3):
-            loads[4 + i].wait()
-            x = sq[i]
-            sq2[i, :, pl.ds(0, SIDE)] = x
-
-        for i in range(3):
-            x = sq2[i]
-            sq2[i] = jnp.where(lanes_of((SIDE, LANES)) < SIDE, x, pltpu.roll(x, SIDE, 1))
-
-        for i in range(3):
-            @pl.loop(0, NV // 8)
-            def _(k, i=i):
-                for j in range(8):
-                    v = k * 8 + j
-                    row = jnp.where(low1, sq2[i, pl.ds(2 * v, 1), :], sq2[i, pl.ds(2 * v + 1, 1), :])
-                    flat[i, :, chunk(v)] = jnp.broadcast_to(row, (8, LANES))
-
-        loads[2].wait()
-        loads[3].wait()
-        diag = lax.broadcasted_iota(I32, (levels, levels), 0) == lax.broadcasted_iota(I32, (levels, levels), 1)
-        for i, col in ((0, kcol), (1, pcol)):
-            column = jnp.sum(jnp.where(diag, jnp.broadcast_to(kp[i], (levels, levels)), 0.0), axis=1, keepdims=True)
-            col[...] = jnp.zeros((rows, LANES), F32)
-            col[pl.ds(0, levels), :] = jnp.broadcast_to(column, (levels, LANES))
-        inv = 1.0 / jnp.sum(kp[0], axis=1, keepdims=True)
-        inv8 = jnp.broadcast_to(inv, (8, LANES))
-
-
-        sset[pl.ds(0, packed), :] = squeeze(
-            jnp.concatenate([roll(cy[:, chunk(1)], SIDE), cy[:, chunk(0)]], axis=1)
-        )
-        sset[pl.ds(packed + 4, 4), :] = jnp.zeros((4, LANES), F32)
-        for i in range(2):
-            for v in range(2):
-                sset[pl.ds(packed + 2 * i + v, 1), :] = flat[1 + i, pl.ds(0, 1), chunk(v)]
-        sets = []
-        for d in range(2):
-            copy = pltpu.make_async_remote_copy(
-                src_ref=sset, dst_ref=rset.at[d], send_sem=sset_sem.at[d], recv_sem=rset_sem.at[d],
-                device_id=(w, bwd(off_y[d])), device_id_type=MESH,
-            )
-            copy.start()
-            sets.append(copy)
 
         @pl.loop(0, tiles_of)
         def _(i):
@@ -778,7 +780,6 @@
             dma((2, windows)),
             dma((windows - 1,)),
             dma((windows - 1,)),
-            pltpu.SemaphoreType.REGULAR,
         ],
         compiler_params=pltpu.CompilerParams(collective_id=0, has_side_effects=True),
     )(

time: 35.8 us -> 33.3 us (0.930)
  Pallas kernels: 35.1 us -> 32.6 us
    pallas_call x1, Pallas kernels: 35.1 us -> 32.6 us  [body(): pl.pallas_call(run, out_shape=pltpu.VMEM((1, 2 * per, SIDE), F32), in_spe...]
where the time goes in v4:
time: 33.3 us; the launch traced here: 33.2 us
  Pallas kernels  32.6 us (98%)
  local copies, waits for them, and re-layouts  0.6 us (2%)
    pallas_call x1, Pallas kernels, body(): pl.pallas_call(run, out_shape=pltpu.VMEM((1, 2 * per, SIDE), F32), in_spe...  32.6 us

profile of v4, /device:TPU:1, one launch (start us, length us, event | category | flops | bytes accessed | tf_op | source)
XLA Modules:
  0.0 33.2 jit_solution(11488046868012453767)
XLA Ops:
  0.0 32.6 %shard_map.91 = f32[1,16,64]{2,1,0:T(8,128)S(1)} custom-call(f32[1152,128]{1,0:T(8,128)} %bitcast.3, bf16[1,1,36,4096]{3,2,1,0:T(8,128)(2,1)} %cx_h.1, bf16[1,1,36,4096]{3,2,1,0:T(8,128)(2,1)} %cy_h.1, f32[1,1,64,64]{3,2,1,0:T(8,128)} %obs_h.1, f32[1,1,64,64]{3,2,1,0:T(8,128)} %pre_h.1, f32[1,36]{1,0:T(1,128)} %bitcast.4, f32[1,36]{1,0:T(1,128)} %bitcast.5, ...), custom_call_target="tpu_custom_call" | custom-call | tf_op jit(solution)/shard_map/pallas_call | solution.py:725
  32.6 0.6 %copy.11 = f32[1,16,64]{2,1,0:T(8,128)} copy(f32[1,16,64]{2,1,0:T(8,128)S(1)} %shard_map.91) | data formatting | bytes 8192

commit v5 on v4

--- a/solution.py
+++ b/solution.py
@@ -145,12 +145,34 @@
                             cols = (cols_key(kind, half) ^ flip) + away
                             mat[pl.ds(src * 256, 256), pl.ds(d * 256 + half * LANES, LANES)] = hot(row_keys[src] == cols)
 
-        def permute(x, mat):
+        def permute(x, mat, first=0):
             top = x.astype(BF16).astype(F32)
             both = jnp.concatenate([top, x - top], axis=0).astype(BF16)
-            res = jnp.dot(both, mat[...], preferred_element_type=F32)
+            res = jnp.dot(both, mat[pl.ds(first, x.shape[1]), :], preferred_element_type=F32)
             n = x.shape[0]
             return res[:n] + res[n:]
+
+        def roll2(x, shift):
+            return jnp.concatenate([roll(x[:, :LANES], shift), roll(x[:, LANES:], shift)], axis=1)
+
+        hide = tiles_of >= 4 and 0 < levels % 8 <= 4
+
+        def tuck(x):
+            if not hide:
+                return x
+            free = (lanes_of((8, 256)) & 3) == 3
+            tail = x[rows - 8 :]
+            heads = [jnp.where(free, roll2(tail, 3 - i), x[8 * i : 8 * i + 8]) for i in range(3)]
+            return jnp.concatenate(heads + [x[24 : rows - 8]], axis=0)
+
+        def untuck(x):
+            if not hide:
+                return x
+            place = lanes_of((8, 256)) & 3
+            tail = jnp.zeros((8, 256), F32)
+            for i in range(3):
+                tail = jnp.where(place == i, roll2(x[8 * i : 8 * i + 8], i - 3), tail)
+            return jnp.concatenate([x, tail], axis=0)
 
         def send(stage, d, to):
             copy = pltpu.make_async_remote_copy(
@@ -162,16 +184,6 @@
             return copy
 
         pending = []
-
-        def send_strips(stage, east, north, mat, offs):
-            res = permute(jnp.concatenate([east, north], axis=1), mat)
-            copies = []
-            for d in range(2):
-                sbuf[stage, d] = res[:, d * 256 : (d + 1) * 256]
-            for d in range(2):
-                copies.append(send(stage, d, fwd(offs[d])))
-            pending.extend(copies)
-            return copies
 
         pairs, odd = tiles_of // 2, tiles_of % 2
         fold = odd == 1 and 0 < levels % 8 <= 4
@@ -209,10 +221,7 @@
         def received(copies, stage):
             for copy in copies:
                 copy.wait_recv()
-            return rbuf[stage, 0] + rbuf[stage, 1]
-
-        def roll2(x, shift):
-            return jnp.concatenate([roll(x[:, :LANES], shift), roll(x[:, LANES:], shift)], axis=1)
+            return untuck(rbuf[stage, 0] + rbuf[stage, 1])
 
         slot8 = jnp.where((l64_8 & 3) < 3, l64_8 >> 2, -1)
 
@@ -250,7 +259,7 @@
 
         strips = permute(jnp.concatenate([epack[...], q[:, pl.ds(CELLS - 256, 256)]], axis=1), wx)
         for d in range(2):
-            sbuf[0, d] = strips[:, d * 256 : (d + 1) * 256]
+            sbuf[0, d] = tuck(strips[:, d * 256 : (d + 1) * 256])
         pl.semaphore_wait(barrier, len(partners))
         first = [send(0, d, fwd(off_x[d])) for d in range(2)]
         pending.extend(first)
@@ -403,13 +412,12 @@
         def tall(x):
             return jnp.concatenate([x] * (rows // 8), axis=0)
 
+        before = permute(jnp.concatenate([epack[...], bx[:, pl.ds(CELLS, 256)]], axis=1), wy)
         panel = received(first, 0)
         dbuf[...] = west_change(panel)
         change = dbuf[:, pl.ds(LANES, LANES)]
-        ends_now = [
-            bx[:, chunk(v + 2)] + jnp.where(l64 < 3, roll(change, -4 * (v % 16)), 0.0) for v in (NV - 2, NV - 1)
-        ]
-        res = permute(jnp.concatenate([epack[...]] + ends_now, axis=1), wy)
+        ends_now = [jnp.where(l64 < 3, roll(change, -4 * (v % 16)), 0.0) for v in (NV - 2, NV - 1)]
+        res = before + permute(jnp.concatenate(ends_now, axis=1), wy, 256)
         for d in range(2):
             sy[d] = squeeze(res[:, d * 256 : (d + 1) * 256])
         y1 = []
@@ -440,16 +448,21 @@
         build(wyt, 3, off_y, 1, True)
         build(wxt, 0, off_x, 0, True)
         pack(cyp, cy, 0, 0)
+        before = permute(jnp.concatenate([epack[...], q[:, pl.ds(CELLS - 256, 256)]], axis=1), wx)
         for copy in y1:
             copy.wait_recv()
         near_two, far_one = unsqueeze(ry[0] + ry[1])
-        east = epack[:, pl.ds(0, LANES)]
+        east = jnp.zeros((rows, LANES), F32)
         for v, res in enumerate(y_first(far_one, near_two)):
             q[:, chunk(v)] = res
             east = jnp.where(((l64 >> 2) == v) & ((l64 & 3) < 3), roll(res, 4 * v - 61), east)
-        epack[:, pl.ds(0, LANES)] = east
-
-        x2 = send_strips(2, epack[...], q[:, pl.ds(CELLS - 256, 256)], wx, off_x)
+        epack[:, pl.ds(0, LANES)] = epack[:, pl.ds(0, LANES)] + east
+        strips = before + permute(east, wx)
+
+        for d in range(2):
+            sbuf[2, d] = tuck(strips[:, d * 256 : (d + 1) * 256])
+        x2 = [send(2, d, fwd(off_x[d])) for d in range(2)]
+        pending.extend(x2)
         x_interior()
         for copy in sets:
             copy.wait_recv()
@@ -498,13 +511,12 @@
         k_all = kcol[...]
         zero = jnp.zeros((rows, LANES), F32)
 
+        before = permute(jnp.concatenate([epack[...], bx[:, pl.ds(CELLS, 256)]], axis=1), wy)
         panel = received(x2, 2)
         dbuf[...] = west_change(panel)
         change = dbuf[:, pl.ds(LANES, LANES)]
-        ends_now = [
-            bx[:, chunk(v + 2)] + jnp.where(l64 < 3, roll(change, -4 * (v % 16)), 0.0) for v in (NV - 2, NV - 1)
-        ]
-        panels = permute(jnp.concatenate([epack[...]] + ends_now, axis=1), wy)
+        ends_now = [jnp.where(l64 < 3, roll(change, -4 * (v % 16)), 0.0) for v in (NV - 2, NV - 1)]
+        panels = before + permute(jnp.concatenate(ends_now, axis=1), wy, 256)
 
         def misfit_weight(col, v_obs, v_pre):
             return v_pre * (col * inv8 - v_obs) * inv8
@@ -754,8 +766,8 @@
             vm((rows, 256), F32),
             vm((rows, 256), F32),
             vm((rows, 256), F32),
-            vm((4, 2, rows, 256), F32),
-            vm((4, 2, rows, 256), F32),
+            vm((4, 2, rows - 8 * (tiles_of >= 4 and 0 < levels % 8 <= 4), 256), F32),
+            vm((4, 2, rows - 8 * (tiles_of >= 4 and 0 < levels % 8 <= 4), 256), F32),
             vm((2, packed, LANES), F32),
             vm((2, packed, LANES), F32),
             vm((2, 1, 256), F32),

time: 33.3 us -> 33.2 us (level)
  no operation moved by 1% of the time
where the time goes in v5:
time: 33.2 us; the launch traced here: 33.1 us
  Pallas kernels  32.5 us (98%)
  local copies, waits for them, and re-layouts  0.6 us (2%)
    pallas_call x1, Pallas kernels, body(): pl.pallas_call(run, out_shape=pltpu.VMEM((1, 2 * per, SIDE), F32), in_spe...  32.5 us

profile of v5, /device:TPU:1, one launch (start us, length us, event | category | flops | bytes accessed | tf_op | source)
XLA Modules:
  0.0 33.1 jit_solution(14579839715569535080)
XLA Ops:
  0.0 32.5 %shard_map.91 = f32[1,16,64]{2,1,0:T(8,128)S(1)} custom-call(f32[1152,128]{1,0:T(8,128)} %bitcast.3, bf16[1,1,36,4096]{3,2,1,0:T(8,128)(2,1)} %cx_h.1, bf16[1,1,36,4096]{3,2,1,0:T(8,128)(2,1)} %cy_h.1, f32[1,1,64,64]{3,2,1,0:T(8,128)} %obs_h.1, f32[1,1,64,64]{3,2,1,0:T(8,128)} %pre_h.1, f32[1,36]{1,0:T(1,128)} %bitcast.4, f32[1,36]{1,0:T(1,128)} %bitcast.5, ...), custom_call_target="tpu_custom_call" | custom-call | tf_op jit(solution)/shard_map/pallas_call | solution.py:737
  32.5 0.6 %copy.11 = f32[1,16,64]{2,1,0:T(8,128)} copy(f32[1,16,64]{2,1,0:T(8,128)S(1)} %shard_map.91) | data formatting | bytes 8192
